TPU v7x, 256 devices: a whole 4x4x8 slice. The times are simulated.
256 devices in a mesh: ctx: 32 (over x, z), head: 8 (over y, core).
Axes of the slice: x: 4, y: 4, z: 8, core: 2. Of those that a mesh axis runs over, the one named last changes fastest.
Arguments:
- queries: bfloat16 [8192, 32, 128], P('ctx', 'head'), may hold values from -40 to 40
- keys: bfloat16 [8192, 8, 128], P('ctx', 'head'), may hold values from -40 to 40
- values: bfloat16 [8192, 8, 128], P('ctx', 'head'), may hold values from -6 to 6
- doc_ids: int32 [8192], P('ctx'), may hold values from 0 to 3, never falling along the last dimension, each value on 1 to 4096 neighbouring positions
Outputs:
- attended: bfloat16 [8192, 4096], P(('ctx', 'head'))
Inputs may be any that keep to these rules, and one draw needn't show every extreme that they name: `doc_ids`: document numbers never fall along the sequence; each document has 1 to 4096 tokens and one has exactly 4096.
All inputs are finite; a program needn't handle non-finite values.
Results may differ from a plain program's by a relative error of at most 0.009.
Values may be sent and summed in bfloat16 or wider, within the bound.
No kernel may reach another device: no remote copies, remote signals or barrier semaphores. Data moves between devices by JAX's collectives and lax.ppermute only.
A program may use at most 128 MiB of HBM per device.

v0:
```python
import functools
import math

import jax
import jax.numpy as jnp
from jax import lax
from jax.experimental import pallas as pl
from jax.experimental.pallas import tpu as pltpu
from jax.sharding import Mesh
from jax.sharding import PartitionSpec as P


TOK = 256
D = 128
HEADS = 4
NZ = 8
NX = 4
HALF = 128
NEG = -1e30
SHIFTS = (0, 2, -2, 4, 1, -1, 3, -3)
NEAR = 3
MIB = 1 << 20
ROWS = TOK * HEADS
GROUPS = ROWS // HALF
SCALE = D**-0.5
SCALE2 = SCALE * math.log2(math.e)
VM = pl.BlockSpec(memory_space=pltpu.VMEM)


def prep_kernel(k_ref, v_ref, ids_ref, kv_ref, cnt_ref):
    kv_ref[0:TOK, :] = k_ref[...]
    kv_ref[TOK : 2 * TOK, :] = v_ref[...]
    ids = ids_ref[...]
    row = lax.broadcasted_iota(jnp.int32, (8, D), 0)
    cnt = jnp.zeros((8, D), jnp.float32)
    for d in (1, 2, 3):
        n = jnp.sum(jnp.where(ids < d, 1.0, 0.0))
        cnt = jnp.where(row == d, n, cnt)
    cnt = cnt.astype(jnp.bfloat16)
    kv_ref[2 * TOK : 2 * TOK + 8, :] = cnt
    cnt_ref[...] = cnt


def prep(k, v, ids):
    return pl.pallas_call(
        prep_kernel,
        out_shape=[
            jax.ShapeDtypeStruct((2 * TOK + 8, D), jnp.bfloat16),
            jax.ShapeDtypeStruct((8, D), jnp.bfloat16),
        ],
        in_specs=[VM] * 3,
        out_specs=[VM] * 2,
        compiler_params=pltpu.CompilerParams(vmem_limit_bytes=4 * MIB),
    )(k, v, ids)


def attn_kernel(deltas, shifts, merge, last, *refs):
    n, nb = len(deltas), len(shifts)
    kv, refs = refs[:nb], refs[nb:]
    qs, refs = refs[:n], refs[n:]
    before, refs = (refs[: 3 * n], refs[3 * n :]) if merge else (None, refs)
    per = {"state": 3, "send": 1, "keep": 2}[last]
    outs, (kscr, vscr, sscr, acc, mscr, lscr, rows_scr, cscr) = refs[: per * n], refs[per * n :]
    x, z = lax.axis_index("x"), lax.axis_index("z")
    for i, ref in enumerate(kv):
        kscr[i] = ref[0:TOK, :]
        vscr[i] = ref[TOK : 2 * TOK, :]
        cnt = ref[2 * TOK : 2 * TOK + 8, :].astype(jnp.float32)
        cscr[i, 0] = lax.rem(z - shifts[i] + NZ, NZ)
        for d in (1, 2, 3):
            cscr[i, d] = jnp.max(cnt[d : d + 1, :]).astype(jnp.int32)

    for j, delta in enumerate(deltas):
        q_ref = qs[j]
        cnt = q_ref[ROWS : ROWS + 8, :].astype(jnp.float32)
        ends = [jnp.max(cnt[d : d + 1, :]).astype(jnp.int32) for d in (1, 2, 3)]

        def pick(tok, a, b, c, d, ends=ends):
            return jnp.where(
                tok >= ends[2], d, jnp.where(tok >= ends[1], c, jnp.where(tok >= ends[0], b, a))
            )

        def bounds(i, tok, delta=delta, pick=pick):
            c1, c2, c3 = cscr[i, 1], cscr[i, 2], cscr[i, 3]
            lo = pick(tok, jnp.int32(0), c1, c2, c3)
            hi = pick(tok, c1, c2, c3, jnp.int32(TOK))
            if delta == 0:
                b = cscr[i, 0]
                hi = jnp.minimum(hi, jnp.where(b < z, TOK, jnp.where(b == z, tok + 1, 0)))
            else:
                hi = jnp.where(x + delta < NX, hi, 0)
            return lo, hi

        def state(i, bounds=bounds):
            lo_a, hi_a = bounds(i, 0)
            lo_b, hi_b = bounds(i, TOK - 1)
            seen = hi_b > lo_a
            whole = (lo_b <= 0) & (hi_a >= TOK)
            return jnp.where(seen, jnp.where(whole, 2, 1), 0)

        def scores(masked, i, q_ref=q_ref, bounds=bounds):
            s = lax.dot_general(
                q_ref[0:ROWS, :],
                kscr[i],
                (((1,), (1,)), ((), ())),
                preferred_element_type=jnp.float32,
            )
            if masked:
                tok = lax.broadcasted_iota(jnp.int32, (TOK, TOK), 0)
                pos = lax.broadcasted_iota(jnp.int32, (TOK, TOK), 1)
                lo, hi = bounds(i, tok)
                seen = (pos >= lo) & (pos < hi)
                s = jnp.concatenate(
                    [jnp.where(seen, s[h * TOK : (h + 1) * TOK], NEG) for h in range(HEADS)],
                    axis=0,
                )
            sscr[i] = s
            mscr[...] = jnp.maximum(mscr[...], jnp.maximum(s[:, 0:D], s[:, D : 2 * D]))

        def first_pass(i, _, state=state, scores=scores):
            st = state(i)
            pl.when(st == 1)(lambda: scores(True, i))
            pl.when(st == 2)(lambda: scores(False, i))
            return 0

        mscr[...] = before[3 * j + 1][...] if merge else jnp.full((ROWS, D), NEG, jnp.float32)
        lax.fori_loop(0, nb, first_pass, 0)
        m = jnp.max(mscr[...], axis=1, keepdims=True)
        if merge:
            shrink = jnp.exp2((before[3 * j + 1][...] - m) * SCALE2)
            acc[...] = before[3 * j][...] * shrink
            lscr[...] = before[3 * j + 2][...] * shrink
        else:
            acc[...] = jnp.zeros_like(acc)
            lscr[...] = jnp.zeros_like(lscr)
        mscr[...] = jnp.broadcast_to(m, (ROWS, D))

        def weigh(i):
            s = sscr[i]
            top = mscr[...]
            lo = jnp.exp2((s[:, 0:D] - top) * SCALE2)
            hi = jnp.exp2((s[:, D : 2 * D] - top) * SCALE2)
            lscr[...] += lo + hi
            p = jnp.concatenate([lo.astype(jnp.bfloat16), hi.astype(jnp.bfloat16)], axis=1)
            acc[...] += jnp.dot(p, vscr[i], preferred_element_type=jnp.float32)

        def second_pass(i, _, state=state):
            pl.when(state(i) > 0)(lambda: weigh(i))
            return 0

        lax.fori_loop(0, nb, second_pass, 0)
        if last == "state":
            outs[3 * j][...] = acc[...]
            outs[3 * j + 1][...] = mscr[...]
            outs[3 * j + 2][...] = lscr[...]
            continue
        total = jnp.maximum(jnp.sum(lscr[...], axis=1, keepdims=True), 1e-30)
        outs[per * j][0:ROWS, :] = (acc[...] * (1.0 / total)).astype(outs[per * j].dtype)
        lse = jnp.broadcast_to(m * SCALE + jnp.log(total), (ROWS, D))
        for g in range(GROUPS):
            rows_scr[g : g + 1, :] = lse[g * HALF : (g + 1) * HALF, :].T[0:1, :]
        if last == "keep":
            outs[2 * j + 1][...] = rows_scr[...]
        elif last == "send":
            rest = rows_scr[...]
            for t in range(3):
                part = rest.astype(jnp.bfloat16)
                outs[j][ROWS + t * GROUPS : ROWS + (t + 1) * GROUPS, :] = part
                rest = rest - part.astype(jnp.float32)


def attn(deltas, shifts, kv, qs, before, last):
    n, nb = len(deltas), len(shifts)
    args = (*kv, *qs, *before)
    wide = jax.ShapeDtypeStruct((ROWS, D), jnp.float32)
    outs = {
        "state": [wide] * 3,
        "send": [jax.ShapeDtypeStruct((ROWS + 3 * GROUPS, D), jnp.bfloat16)],
        "keep": [wide, jax.ShapeDtypeStruct((GROUPS, D), jnp.float32)],
    }[last] * n
    return pl.pallas_call(
        functools.partial(attn_kernel, deltas, shifts, bool(before), last),
        out_shape=outs,
        in_specs=[VM] * len(args),
        out_specs=[VM] * len(outs),
        scratch_shapes=[
            pltpu.VMEM((nb, TOK, D), jnp.bfloat16),
            pltpu.VMEM((nb, TOK, D), jnp.bfloat16),
            pltpu.VMEM((nb, ROWS, TOK), jnp.float32),
            pltpu.VMEM((ROWS, D), jnp.float32),
            pltpu.VMEM((ROWS, D), jnp.float32),
            pltpu.VMEM((ROWS, D), jnp.float32),
            pltpu.VMEM((GROUPS, D), jnp.float32),
            pltpu.SMEM((nb, 4), jnp.int32),
        ],
        compiler_params=pltpu.CompilerParams(vmem_limit_bytes=20 * MIB),
        cost_estimate=pl.CostEstimate(
            flops=4 * ROWS * D * TOK * nb * n,
            bytes_accessed=MIB,
            transcendentals=ROWS * TOK * nb * n,
        ),
    )(*args)


def combine_kernel(a_ref, lse_ref, b_ref, c_ref, o_ref):
    x = lax.axis_index("x")

    def lse_of(ref, delta):
        terms = [
            ref[ROWS + t * GROUPS : ROWS + (t + 1) * GROUPS, :].astype(jnp.float32)
            for t in range(3)
        ]
        return jnp.where(x >= delta, terms[0] + (terms[1] + terms[2]), NEG)

    lses = (lse_ref[...], lse_of(b_ref, 1), lse_of(c_ref, 2))
    top = jnp.maximum(jnp.maximum(lses[0], lses[1]), lses[2])
    ws = [jnp.exp(lse - top) for lse in lses]
    inv = 1.0 / (ws[0] + ws[1] + ws[2])
    pad = jnp.zeros((HALF - GROUPS, D), jnp.float32)
    ws = [jnp.concatenate([w * inv, pad], axis=0).T for w in ws]
    for g in range(GROUPS):
        h, u = divmod(g, TOK // HALF)
        rows = slice(g * HALF, (g + 1) * HALF)
        o = sum(
            ref[rows, :].astype(jnp.float32) * w[:, g : g + 1]
            for ref, w in zip((a_ref, b_ref, c_ref), ws)
        )
        o_ref[u * HALF : (u + 1) * HALF, h * D : (h + 1) * D] = o.astype(o_ref.dtype)


def combine(*args):
    return pl.pallas_call(
        combine_kernel,
        out_shape=jax.ShapeDtypeStruct((TOK, HEADS * D), jnp.bfloat16),
        in_specs=[VM] * len(args),
        out_specs=VM,
        compiler_params=pltpu.CompilerParams(vmem_limit_bytes=6 * MIB),
    )(*args)


def along(a, axis, shift, n):
    pairs = [(i, i + shift) for i in range(n)]
    if axis == "x":
        pairs = [(i, j) for i, j in pairs if 0 <= j < n]
    return lax.ppermute(a, axis, [(i, j % n) for i, j in pairs])


def local(queries, keys, values, doc_ids):
    kv, counts = prep(keys.reshape(TOK, D), values.reshape(TOK, D), doc_ids.reshape(2, D))
    q = jnp.transpose(queries, (1, 0, 2)).reshape(ROWS, D)
    q = jnp.concatenate([q, counts], axis=0)

    up2 = along(kv, "z", 2, NZ)
    dn2 = along(kv, "z", -2, NZ)
    q2 = along(q, "x", -2, NX)
    q1 = along(q, "x", -1, NX)
    far = along(kv, "z", 4, NZ)
    up3 = along(up2, "z", 1, NZ)
    dn3 = along(dn2, "z", -1, NZ)
    up1 = along(kv, "z", 1, NZ)
    dn1 = along(kv, "z", -1, NZ)
    blocks = [kv, up2, dn2, far, up1, dn1, up3, dn3]
    near = attn((2, 1), SHIFTS[:NEAR], blocks[:NEAR], [q2, q1], (), "state")
    (o2,) = attn((2,), SHIFTS[NEAR:], blocks[NEAR:], [q2], near[:3], "send")
    r2 = along(o2, "x", 2, NX)
    (o1,) = attn((1,), SHIFTS[NEAR:], blocks[NEAR:], [q1], near[3:], "send")
    r1 = along(o1, "x", 1, NX)
    o0, lse0 = attn((0,), SHIFTS, blocks, [q], (), "keep")
    merged = combine(o0, lse0, r1, r2)
    return lax.all_to_all(merged, ("y", "core"), split_axis=0, concat_axis=1, tiled=True)


def solution(mesh):
    grid = Mesh(mesh.devices.reshape(NX, NZ, 4, 2), ("x", "z", "y", "core"))
    ctx, head = ("x", "z"), ("y", "core")
    return jax.shard_map(
        local,
        mesh=grid,
        in_specs=(P(ctx, head, None), P(ctx, head, None), P(ctx, head, None), P(ctx)),
        out_specs=P(ctx + head, None),
        check_vma=False,
    )
```

profile of v0, /device:TPU:1, one launch (start us, length us, event | category | flops | bytes accessed | tf_op | source)
XLA Modules:
  0.0 63.7 jit_solution(16059271851292133035)
XLA Ops:
  0.0 1.0 %copy.5 = bf16[4,256,128]{2,1,0:T(8,128)(2,1)S(1)} copy(bf16[4,256,128]{2,0,1:T(4,128)(2,1)} %bitcast.15) | data formatting | bytes 524288 | tf_op jit(solution)/shard_map/transpose | solution.py:250
  1.0 0.0 copy-start.2
  1.1 0.7 %copy-done.2 = s32[256]{0:T(256)S(1)} copy-done((s32[256]{0:T(256)S(1)}, s32[256]{0:T(256)}, u32[]{:S(2)}) %copy-start.2) | copy-done | bytes 1048
  1.7 0.1 shard_map.46
  1.9 1.3 %collective-permute-start.8 = (bf16[1032,128]{1,0:T(8,128)(2,1)S(1)}, bf16[1032,128]{1,0:T(8,128)(2,1)S(1)}, u32[]{:S(2)}, u32[]{:S(2)}) collective-permute-start(bf16[1032,128]{1,0:T(8,128)(2,1)S(1)} %pad_maximum_fusion.refs_8_), channel_id=1, source_target_pairs={{128,0},{192,64},{129,1},{193,65},{130,2},{194,66},{131,3},{195,67... | collective-permute-start | bytes 792584 | tf_op jit(solution)/shard_map/ppermute | solution.py:245
  3.2 1.3 %collective-permute-start.7 = (bf16[1032,128]{1,0:T(8,128)(2,1)S(1)}, bf16[1032,128]{1,0:T(8,128)(2,1)S(1)}, u32[]{:S(2)}, u32[]{:S(2)}) collective-permute-start(bf16[1032,128]{1,0:T(8,128)(2,1)S(1)} %pad_maximum_fusion.refs_8_), channel_id=1, source_target_pairs={{64,0},{128,64},{192,128},{65,1},{129,65},{193,129},{66,2},{130,66... | collective-permute-start | bytes 792584 | tf_op jit(solution)/shard_map/ppermute | solution.py:245
  4.5 6.9 %collective-permute-start.1 = (bf16[520,128]{1,0:T(8,128)(2,1)S(1)}, bf16[520,128]{1,0:T(8,128)(2,1)S(1)}, u32[]{:S(2)}, u32[]{:S(2)}) collective-permute-start(bf16[520,128]{1,0:T(8,128)(2,1)S(1)} %get-tuple-element.15.refs_0_), channel_id=1, source_target_pairs={{0,48},{8,56},{16,0},{24,8},{32,16},{40,24},{48,32},{56,40},{1,49}... | collective-permute-start | bytes 399368 | tf_op jit(solution)/shard_map/ppermute | solution.py:245
  11.4 0.0 collective-permute-start
  11.4 3.1 %collective-permute-start.4 = (bf16[520,128]{1,0:T(8,128)(2,1)S(1)}, bf16[520,128]{1,0:T(8,128)(2,1)S(1)}, u32[]{:S(2)}, u32[]{:S(2)}) collective-permute-start(bf16[520,128]{1,0:T(8,128)(2,1)S(1)} %get-tuple-element.15.refs_0_), channel_id=1, source_target_pairs={{0,56},{8,0},{16,8},{24,16},{32,24},{40,32},{48,40},{56,48},{1,57}... | collective-permute-start | bytes 399368 | tf_op jit(solution)/shard_map/ppermute | solution.py:245
  14.5 0.4 collective-permute-done.1.refs_2_
  14.9 1.6 %collective-permute-start.3 = (bf16[520,128]{1,0:T(8,128)(2,1)S(1)}, bf16[520,128]{1,0:T(8,128)(2,1)S(1)}, u32[]{:S(2)}, u32[]{:S(2)}) collective-permute-start(bf16[520,128]{1,0:T(8,128)(2,1)S(1)} %get-tuple-element.15.refs_0_), channel_id=1, source_target_pairs={{0,8},{8,16},{16,24},{24,32},{32,40},{40,48},{48,56},{56,0},{1,9},... | collective-permute-start | bytes 399368 | tf_op jit(solution)/shard_map/ppermute | solution.py:245
  16.5 2.3 %collective-permute-done.refs_1_ = bf16[520,128]{1,0:T(8,128)(2,1)S(1)} collective-permute-done((bf16[520,128]{1,0:T(8,128)(2,1)S(1)}, bf16[520,128]{1,0:T(8,128)(2,1)S(1)}, u32[]{:S(2)}, u32[]{:S(2)}) %collective-permute-start) | collective-permute-done | bytes 133152 | tf_op jit(solution)/shard_map/ppermute | solution.py:245
  18.7 1.7 %collective-permute-start.2 = (bf16[520,128]{1,0:T(8,128)(2,1)S(1)}, bf16[520,128]{1,0:T(8,128)(2,1)S(1)}, u32[]{:S(2)}, u32[]{:S(2)}) collective-permute-start(bf16[520,128]{1,0:T(8,128)(2,1)S(1)} %get-tuple-element.15.refs_0_), channel_id=1, source_target_pairs={{0,32},{8,40},{16,48},{24,56},{32,0},{40,8},{48,16},{56,24},{1,33}... | collective-permute-start | bytes 399368 | tf_op jit(solution)/shard_map/ppermute | solution.py:245
  20.4 0.0 collective-permute-done.8.refs_3_.refs_5_
  20.4 2.7 %collective-permute-start.6 = (bf16[520,128]{1,0:T(8,128)(2,1)S(1)}, bf16[520,128]{1,0:T(8,128)(2,1)S(1)}, u32[]{:S(2)}, u32[]{:S(2)}) collective-permute-start(bf16[520,128]{1,0:T(8,128)(2,1)S(1)} %collective-permute-done.1.refs_2_), channel_id=1, source_target_pairs={{0,56},{8,0},{16,8},{24,16},{32,24},{40,32},{48,40},{56,48},{1,57}... | collective-permute-start | bytes 399368 | tf_op jit(solution)/shard_map/ppermute | solution.py:245
  23.1 0.0 collective-permute-done.7.refs_4_.refs_5_
  23.1 0.4 collective-permute-start.5
  23.5 1.1 %shard_map.48 = (f32[1024,128]{1,0:T(8,128)S(1)}, f32[1024,128]{1,0:T(8,128)S(1)}, f32[1024,128]{1,0:T(8,128)S(1)}, f32[1024,128]{1,0:T(8,128)S(1)}, f32[1024,128]{1,0:T(8,128)S(1)}, /*index=5*/f32[1024,128]{1,0:T(8,128)S(1)}) custom-call(bf16[520,128]{1,0:T(8,128)(2,1)S(1)} %get-tuple-element.15.refs_0_, bf16[520,128]{1,0:T(8,128)(2,1)S(1)} %collective-permute-done.refs_1_, ...), custom_call_target="tpu_custom_call" | custom-call | flops 805306368 | bytes 1048576 | tf_op jit(solution)/shard_map/pallas_call | solution.py:181
  24.7 0.0 collective-permute-done.4.refs_5_.refs_2_
  24.7 0.0 collective-permute-done.3.refs_4_.refs_1_
  24.7 2.3 %collective-permute-done.2.refs_3_.refs_0_ = bf16[520,128]{1,0:T(8,128)(2,1)S(1)} collective-permute-done((bf16[520,128]{1,0:T(8,128)(2,1)S(1)}, bf16[520,128]{1,0:T(8,128)(2,1)S(1)}, u32[]{:S(2)}, u32[]{:S(2)}) %collective-permute-start.2) | collective-permute-done | bytes 133152 | tf_op jit(solution)/shard_map/ppermute | solution.py:245
  26.9 5.5 %collective-permute-done.6.refs_7_.refs_4_ = bf16[520,128]{1,0:T(8,128)(2,1)S(1)} collective-permute-done((bf16[520,128]{1,0:T(8,128)(2,1)S(1)}, bf16[520,128]{1,0:T(8,128)(2,1)S(1)}, u32[]{:S(2)}, u32[]{:S(2)}) %collective-permute-start.6) | collective-permute-done | bytes 133152 | tf_op jit(solution)/shard_map/ppermute | solution.py:245
  32.4 0.0 collective-permute-done.5.refs_6_.refs_3_
  32.4 1.0 %shard_map.50 = bf16[1048,128]{1,0:T(8,128)(2,1)S(1)} custom-call(bf16[520,128]{1,0:T(8,128)(2,1)S(1)} %collective-permute-done.2.refs_3_.refs_0_, bf16[520,128]{1,0:T(8,128)(2,1)S(1)} %collective-permute-done.3.refs_4_.refs_1_, bf16[520,128]{1,0:T(8,128)(2,1)S(1)} %collective-permute-done.4.refs_5_.refs_2_, ...), custom_call_target="tpu_custom_call" | custom-call | flops 671088640 | bytes 1048576 | tf_op jit(solution)/shard_map/pallas_call | solution.py:181
  33.4 5.8 %collective-permute-start.10 = (bf16[1048,128]{1,0:T(8,128)(2,1)S(1)}, bf16[1048,128]{1,0:T(8,128)(2,1)S(1)}, u32[]{:S(2)}, u32[]{:S(2)}) collective-permute-start(bf16[1048,128]{1,0:T(8,128)(2,1)S(1)} %shard_map.50), channel_id=1, source_target_pairs={{0,128},{64,192},{1,129},{65,193},{2,130},{66,194},{3,131},{67,195... | collective-permute-start | bytes 804872 | tf_op jit(solution)/shard_map/ppermute | solution.py:245
  39.2 1.6 %shard_map.49 = bf16[1048,128]{1,0:T(8,128)(2,1)S(1)} custom-call(bf16[520,128]{1,0:T(8,128)(2,1)S(1)} %collective-permute-done.2.refs_3_.refs_0_, bf16[520,128]{1,0:T(8,128)(2,1)S(1)} %collective-permute-done.3.refs_4_.refs_1_, bf16[520,128]{1,0:T(8,128)(2,1)S(1)} %collective-permute-done.4.refs_5_.refs_2_, ...), custom_call_target="tpu_custom_call" | custom-call | flops 671088640 | bytes 1048576 | tf_op jit(solution)/shard_map/pallas_call | solution.py:181
  40.9 1.6 %collective-permute-start.9 = (bf16[1048,128]{1,0:T(8,128)(2,1)S(1)}, bf16[1048,128]{1,0:T(8,128)(2,1)S(1)}, u32[]{:S(2)}, u32[]{:S(2)}) collective-permute-start(bf16[1048,128]{1,0:T(8,128)(2,1)S(1)} %shard_map.49), channel_id=1, source_target_pairs={{0,64},{64,128},{128,192},{1,65},{65,129},{129,193},{2,66},{66,130... | collective-permute-start | bytes 804872 | tf_op jit(solution)/shard_map/ppermute | solution.py:245
  42.5 1.9 %shard_map.47 = (f32[1024,128]{1,0:T(8,128)S(1)}, f32[8,128]{1,0:T(8,128)S(1)}) custom-call(bf16[520,128]{1,0:T(8,128)(2,1)S(1)} %get-tuple-element.15.refs_0_, bf16[520,128]{1,0:T(8,128)(2,1)S(1)} %collective-permute-done.refs_1_, bf16[520,128]{1,0:T(8,128)(2,1)S(1)} %collective-permute-done.1.refs_2_, ...), custom_call_target="tpu_custom_call" | custom-call | flops 1073741824 | bytes 1048576 | tf_op jit(solution)/shard_map/pallas_call | solution.py:181
  44.4 4.8 %collective-permute-done.9.b_ref = bf16[1048,128]{1,0:T(8,128)(2,1)S(1)} collective-permute-done((bf16[1048,128]{1,0:T(8,128)(2,1)S(1)}, bf16[1048,128]{1,0:T(8,128)(2,1)S(1)}, u32[]{:S(2)}, u32[]{:S(2)}) %collective-permute-start.9) | collective-permute-done | bytes 268320 | tf_op jit(solution)/shard_map/ppermute | solution.py:245
  49.2 0.7 %shard_map.51 = bf16[256,512]{1,0:T(8,128)(2,1)S(1)} custom-call(f32[1024,128]{1,0:T(8,128)S(1)} %get-tuple-element.17.a_ref, f32[8,128]{1,0:T(8,128)S(1)} %get-tuple-element.18.lse_ref, bf16[1048,128]{1,0:T(8,128)(2,1)S(1)} %collective-permute-done.9.b_ref, bf16[1048,128]{1,0:T(8,128)(2,1)S(1)} %collective-permute-done.10.c_ref), custom_call_target="tpu_custom_call" | custom-call | tf_op jit(solution)/shard_map/pallas_call | solution.py:232
  49.8 13.2 %all_to_all.19 = bf16[8,32,512]{2,1,0:T(8,128)(2,1)S(1)} all-to-all(bf16[8,32,512]{2,1,0:T(8,128)(2,1)S(1)} %bitcast.9), channel_id=1, replica_groups=mesh['x'=4,'z'=8,'y'=4,'core'=2] {'y','core'}, dimensions={0} | all-to-all | bytes 524288 | tf_op jit(solution)/shard_map/all_to_all | solution.py:270
  63.0 0.7 %copy.7 = bf16[8,4,8,512]{3,2,0,1:T(8,128)(2,1)} copy(bf16[8,4,8,512]{3,2,1,0:T(8,128)(2,1)S(1)} %bitcast.14) | data formatting | bytes 524288 | tf_op jit(solution)/shard_map/all_to_all | solution.py:270
  (6 shorter events, 0.0 us)
Async XLA Ops:
  0.0 1.0 %copy-start = (bf16[256,1,128]{2,0,1:T(8,128)(2,1)S(1)}, bf16[256,1,128]{2,0,1:T(8,128)(2,1)}, u32[]{:S(2)}) copy-start(bf16[256,1,128]{2,0,1:T(8,128)(2,1)} %param.5) | copy-start | bytes 196612
  0.0 1.1 %copy-start.1 = (bf16[256,1,128]{2,0,1:T(8,128)(2,1)S(1)}, bf16[256,1,128]{2,0,1:T(8,128)(2,1)}, u32[]{:S(2)}) copy-start(bf16[256,1,128]{2,0,1:T(8,128)(2,1)} %param.6) | copy-start | bytes 196612
  1.0 0.7 %copy-start.2 = (s32[256]{0:T(256)S(1)}, s32[256]{0:T(256)}, u32[]{:S(2)}) copy-start(s32[256]{0:T(256)} %param.7) | copy-start | bytes 3076
  1.9 18.6 %collective-permute-start.8 = (bf16[1032,128]{1,0:T(8,128)(2,1)S(1)}, bf16[1032,128]{1,0:T(8,128)(2,1)S(1)}, u32[]{:S(2)}, u32[]{:S(2)}) collective-permute-start(bf16[1032,128]{1,0:T(8,128)(2,1)S(1)} %pad_maximum_fusion.refs_8_), channel_id=1, source_target_pairs={{128,0},{192,64},{129,1},{193,65},{130,2},{194,66},{131,3},{195,67... | collective-permute-start | bytes 792584 | tf_op jit(solution)/shard_map/ppermute | solution.py:245
  3.2 19.9 %collective-permute-start.7 = (bf16[1032,128]{1,0:T(8,128)(2,1)S(1)}, bf16[1032,128]{1,0:T(8,128)(2,1)S(1)}, u32[]{:S(2)}, u32[]{:S(2)}) collective-permute-start(bf16[1032,128]{1,0:T(8,128)(2,1)S(1)} %pad_maximum_fusion.refs_8_), channel_id=1, source_target_pairs={{64,0},{128,64},{192,128},{65,1},{129,65},{193,129},{66,2},{130,66... | collective-permute-start | bytes 792584 | tf_op jit(solution)/shard_map/ppermute | solution.py:245
  4.5 10.4 %collective-permute-start.1 = (bf16[520,128]{1,0:T(8,128)(2,1)S(1)}, bf16[520,128]{1,0:T(8,128)(2,1)S(1)}, u32[]{:S(2)}, u32[]{:S(2)}) collective-permute-start(bf16[520,128]{1,0:T(8,128)(2,1)S(1)} %get-tuple-element.15.refs_0_), channel_id=1, source_target_pairs={{0,48},{8,56},{16,0},{24,8},{32,16},{40,24},{48,32},{56,40},{1,49}... | collective-permute-start | bytes 399368 | tf_op jit(solution)/shard_map/ppermute | solution.py:245
  11.4 7.4 %collective-permute-start = (bf16[520,128]{1,0:T(8,128)(2,1)S(1)}, bf16[520,128]{1,0:T(8,128)(2,1)S(1)}, u32[]{:S(2)}, u32[]{:S(2)}) collective-permute-start(bf16[520,128]{1,0:T(8,128)(2,1)S(1)} %get-tuple-element.15.refs_0_), channel_id=1, source_target_pairs={{0,16},{8,24},{16,32},{24,40},{32,48},{40,56},{48,0},{56,8},{1,17}... | collective-permute-start | bytes 399368 | tf_op jit(solution)/shard_map/ppermute | solution.py:245
  11.4 13.3 %collective-permute-start.4 = (bf16[520,128]{1,0:T(8,128)(2,1)S(1)}, bf16[520,128]{1,0:T(8,128)(2,1)S(1)}, u32[]{:S(2)}, u32[]{:S(2)}) collective-permute-start(bf16[520,128]{1,0:T(8,128)(2,1)S(1)} %get-tuple-element.15.refs_0_), channel_id=1, source_target_pairs={{0,56},{8,0},{16,8},{24,16},{32,24},{40,32},{48,40},{56,48},{1,57}... | collective-permute-start | bytes 399368 | tf_op jit(solution)/shard_map/ppermute | solution.py:245
  14.9 9.8 %collective-permute-start.3 = (bf16[520,128]{1,0:T(8,128)(2,1)S(1)}, bf16[520,128]{1,0:T(8,128)(2,1)S(1)}, u32[]{:S(2)}, u32[]{:S(2)}) collective-permute-start(bf16[520,128]{1,0:T(8,128)(2,1)S(1)} %get-tuple-element.15.refs_0_), channel_id=1, source_target_pairs={{0,8},{8,16},{16,24},{24,32},{32,40},{40,48},{48,56},{56,0},{1,9},... | collective-permute-start | bytes 399368 | tf_op jit(solution)/shard_map/ppermute | solution.py:245
  18.7 8.2 %collective-permute-start.2 = (bf16[520,128]{1,0:T(8,128)(2,1)S(1)}, bf16[520,128]{1,0:T(8,128)(2,1)S(1)}, u32[]{:S(2)}, u32[]{:S(2)}) collective-permute-start(bf16[520,128]{1,0:T(8,128)(2,1)S(1)} %get-tuple-element.15.refs_0_), channel_id=1, source_target_pairs={{0,32},{8,40},{16,48},{24,56},{32,0},{40,8},{48,16},{56,24},{1,33}... | collective-permute-start | bytes 399368 | tf_op jit(solution)/shard_map/ppermute | solution.py:245
  20.4 12.0 %collective-permute-start.6 = (bf16[520,128]{1,0:T(8,128)(2,1)S(1)}, bf16[520,128]{1,0:T(8,128)(2,1)S(1)}, u32[]{:S(2)}, u32[]{:S(2)}) collective-permute-start(bf16[520,128]{1,0:T(8,128)(2,1)S(1)} %collective-permute-done.1.refs_2_), channel_id=1, source_target_pairs={{0,56},{8,0},{16,8},{24,16},{32,24},{40,32},{48,40},{56,48},{1,57}... | collective-permute-start | bytes 399368 | tf_op jit(solution)/shard_map/ppermute | solution.py:245
  23.1 9.3 %collective-permute-start.5 = (bf16[520,128]{1,0:T(8,128)(2,1)S(1)}, bf16[520,128]{1,0:T(8,128)(2,1)S(1)}, u32[]{:S(2)}, u32[]{:S(2)}) collective-permute-start(bf16[520,128]{1,0:T(8,128)(2,1)S(1)} %collective-permute-done.refs_1_), channel_id=1, source_target_pairs={{0,8},{8,16},{16,24},{24,32},{32,40},{40,48},{48,56},{56,0},{1,9},... | collective-permute-start | bytes 399368 | tf_op jit(solution)/shard_map/ppermute | solution.py:245
  33.4 11.0 %collective-permute-start.10 = (bf16[1048,128]{1,0:T(8,128)(2,1)S(1)}, bf16[1048,128]{1,0:T(8,128)(2,1)S(1)}, u32[]{:S(2)}, u32[]{:S(2)}) collective-permute-start(bf16[1048,128]{1,0:T(8,128)(2,1)S(1)} %shard_map.50), channel_id=1, source_target_pairs={{0,128},{64,192},{1,129},{65,193},{2,130},{66,194},{3,131},{67,195... | collective-permute-start | bytes 804872 | tf_op jit(solution)/shard_map/ppermute | solution.py:245
  40.9 8.3 %collective-permute-start.9 = (bf16[1048,128]{1,0:T(8,128)(2,1)S(1)}, bf16[1048,128]{1,0:T(8,128)(2,1)S(1)}, u32[]{:S(2)}, u32[]{:S(2)}) collective-permute-start(bf16[1048,128]{1,0:T(8,128)(2,1)S(1)} %shard_map.49), channel_id=1, source_target_pairs={{0,64},{64,128},{128,192},{1,65},{65,129},{129,193},{2,66},{66,130... | collective-permute-start | bytes 804872 | tf_op jit(solution)/shard_map/ppermute | solution.py:245
where the time goes:
time: 64.5 us; the launch traced here: 63.7 us
  starting transfers between devices  26.4 us (41%)
  waiting for transfers between devices  15.2 us (24%)
  blocking collectives  13.2 us (20%)
  Pallas kernels  6.43 us (10%)
  local copies, waits for them, and re-layouts  2.4 us (4%)
    ppermute x11, starting transfers between devices, along(): return lax.ppermute(a, axis, [(i, j % n) for i, j in pairs])  26.4 us
    ppermute x11, waiting for transfers between devices, along(): return lax.ppermute(a, axis, [(i, j % n) for i, j in pairs])  15.2 us
    all_to_all x1, blocking collectives, local(): lax.all_to_all(merged, ('y', 'core'), split_axis=0, concat_axis=1, tiled=...  13.2 us
    pallas_call x4, Pallas kernels, attn(): pl.pallas_call(functools.partial(attn_kernel, deltas, shifts, bool(before...  5.64 us
  transfers between devices with their start and end apart: 11, of which 5 were waited for; matrix products, arithmetic and copies ran while one was open for 0% of the time, Pallas kernels for 7%

commit v1 on v0

--- a/solution.py
+++ b/solution.py
@@ -17,8 +17,10 @@
 NX = 4
 HALF = 128
 NEG = -1e30
-SHIFTS = (0, 2, -2, 4, 1, -1, 3, -3)
-NEAR = 3
+PIECE = 2 * TOK + 8
+NEAR = ((0, 0, 0), (1, 0, 2), (2, 0, -2))
+REST = ((0, 0, 4), (1, 0, 1), (1, PIECE, 3), (2, 0, -1), (2, PIECE, -3))
+EVERY = NEAR + tuple((array + len(NEAR), row, shift) for array, row, shift in REST)
 MIB = 1 << 20
 ROWS = TOK * HEADS
 GROUPS = ROWS // HALF
@@ -27,46 +29,57 @@
 VM = pl.BlockSpec(memory_space=pltpu.VMEM)
 
 
-def prep_kernel(k_ref, v_ref, ids_ref, kv_ref, cnt_ref):
-    kv_ref[0:TOK, :] = k_ref[...]
-    kv_ref[TOK : 2 * TOK, :] = v_ref[...]
-    ids = ids_ref[...]
+def prep_kernel(k_ref, v_ref, ids_ref, kv_ref, cnt_ref, ids, sems):
+    copies = [
+        pltpu.make_async_copy(ids_ref, ids, sems.at[0]),
+        pltpu.make_async_copy(k_ref, kv_ref.at[0:TOK, :], sems.at[1]),
+        pltpu.make_async_copy(v_ref, kv_ref.at[TOK : 2 * TOK, :], sems.at[2]),
+    ]
+    for copy in copies:
+        copy.start()
+    copies[0].wait()
     row = lax.broadcasted_iota(jnp.int32, (8, D), 0)
     cnt = jnp.zeros((8, D), jnp.float32)
     for d in (1, 2, 3):
-        n = jnp.sum(jnp.where(ids < d, 1.0, 0.0))
+        n = jnp.sum(jnp.where(ids[...] < d, 1.0, 0.0))
         cnt = jnp.where(row == d, n, cnt)
     cnt = cnt.astype(jnp.bfloat16)
     kv_ref[2 * TOK : 2 * TOK + 8, :] = cnt
     cnt_ref[...] = cnt
+    for copy in copies[1:]:
+        copy.wait()
 
 
 def prep(k, v, ids):
+    k, v, ids = (pltpu.with_memory_space_constraint(a, pltpu.HBM) for a in (k, v, ids))
     return pl.pallas_call(
         prep_kernel,
         out_shape=[
             jax.ShapeDtypeStruct((2 * TOK + 8, D), jnp.bfloat16),
             jax.ShapeDtypeStruct((8, D), jnp.bfloat16),
         ],
-        in_specs=[VM] * 3,
+        in_specs=[pl.BlockSpec(memory_space=pltpu.HBM)] * 3,
         out_specs=[VM] * 2,
+        scratch_shapes=[pltpu.VMEM((2, D), jnp.int32), pltpu.SemaphoreType.DMA((3,))],
         compiler_params=pltpu.CompilerParams(vmem_limit_bytes=4 * MIB),
     )(k, v, ids)
 
 
-def attn_kernel(deltas, shifts, merge, last, *refs):
-    n, nb = len(deltas), len(shifts)
-    kv, refs = refs[:nb], refs[nb:]
+def attn_kernel(deltas, blocks, merge, last, *refs):
+    n, nb = len(deltas), len(blocks)
+    arrays = 1 + max(array for array, _, _ in blocks)
+    kv, refs = refs[:arrays], refs[arrays:]
     qs, refs = refs[:n], refs[n:]
     before, refs = (refs[: 3 * n], refs[3 * n :]) if merge else (None, refs)
     per = {"state": 3, "send": 1, "keep": 2}[last]
     outs, (kscr, vscr, sscr, acc, mscr, lscr, rows_scr, cscr) = refs[: per * n], refs[per * n :]
     x, z = lax.axis_index("x"), lax.axis_index("z")
-    for i, ref in enumerate(kv):
-        kscr[i] = ref[0:TOK, :]
-        vscr[i] = ref[TOK : 2 * TOK, :]
-        cnt = ref[2 * TOK : 2 * TOK + 8, :].astype(jnp.float32)
-        cscr[i, 0] = lax.rem(z - shifts[i] + NZ, NZ)
+    for i, (array, row, shift) in enumerate(blocks):
+        ref = kv[array]
+        kscr[i] = ref[row : row + TOK, :]
+        vscr[i] = ref[row + TOK : row + 2 * TOK, :]
+        cnt = ref[row + 2 * TOK : row + PIECE, :].astype(jnp.float32)
+        cscr[i, 0] = lax.rem(z - shift + NZ, NZ)
         for d in (1, 2, 3):
             cscr[i, d] = jnp.max(cnt[d : d + 1, :]).astype(jnp.int32)
 
@@ -169,8 +182,8 @@
                 rest = rest - part.astype(jnp.float32)
 
 
-def attn(deltas, shifts, kv, qs, before, last):
-    n, nb = len(deltas), len(shifts)
+def attn(deltas, blocks, kv, qs, before, last):
+    n, nb = len(deltas), len(blocks)
     args = (*kv, *qs, *before)
     wide = jax.ShapeDtypeStruct((ROWS, D), jnp.float32)
     outs = {
@@ -179,7 +192,7 @@
         "keep": [wide, jax.ShapeDtypeStruct((GROUPS, D), jnp.float32)],
     }[last] * n
     return pl.pallas_call(
-        functools.partial(attn_kernel, deltas, shifts, bool(before), last),
+        functools.partial(attn_kernel, deltas, blocks, bool(before), last),
         out_shape=outs,
         in_specs=[VM] * len(args),
         out_specs=[VM] * len(outs),
@@ -255,17 +268,15 @@
     q2 = along(q, "x", -2, NX)
     q1 = along(q, "x", -1, NX)
     far = along(kv, "z", 4, NZ)
-    up3 = along(up2, "z", 1, NZ)
-    dn3 = along(dn2, "z", -1, NZ)
-    up1 = along(kv, "z", 1, NZ)
-    dn1 = along(kv, "z", -1, NZ)
-    blocks = [kv, up2, dn2, far, up1, dn1, up3, dn3]
-    near = attn((2, 1), SHIFTS[:NEAR], blocks[:NEAR], [q2, q1], (), "state")
-    (o2,) = attn((2,), SHIFTS[NEAR:], blocks[NEAR:], [q2], near[:3], "send")
+    up13 = along(jnp.concatenate([kv, up2], axis=0), "z", 1, NZ)
+    dn13 = along(jnp.concatenate([kv, dn2], axis=0), "z", -1, NZ)
+    first, rest = [kv, up2, dn2], [far, up13, dn13]
+    near = attn((1, 2), NEAR, first, [q1, q2], (), "state")
+    (o1,) = attn((1,), REST, rest, [q1], near[:3], "send")
+    r1 = along(o1, "x", 1, NX)
+    (o2,) = attn((2,), REST, rest, [q2], near[3:], "send")
     r2 = along(o2, "x", 2, NX)
-    (o1,) = attn((1,), SHIFTS[NEAR:], blocks[NEAR:], [q1], near[3:], "send")
-    r1 = along(o1, "x", 1, NX)
-    o0, lse0 = attn((0,), SHIFTS, blocks, [q], (), "keep")
+    o0, lse0 = attn((0,), EVERY, first + rest, [q], (), "keep")
     merged = combine(o0, lse0, r1, r2)
     return lax.all_to_all(merged, ("y", "core"), split_axis=0, concat_axis=1, tiled=True)
 

time: 64.5 us -> 60.1 us (0.932)
  the two profiles are of different devices: /device:TPU:1 before, /device:TPU:36 now
where the time goes in v1:
time: 60.1 us; the launch traced here: 59.8 us
  waiting for transfers between devices  17.3 us (29%)
  starting transfers between devices  16.6 us (28%)
  blocking collectives  12.1 us (20%)
  Pallas kernels  12 us (20%)
  local copies, waits for them, and re-layouts  1.71 us (3%)
    ppermute x9, waiting for transfers between devices, along(): return lax.ppermute(a, axis, [(i, j % n) for i, j in pairs])  17.3 us
    ppermute x9, starting transfers between devices, along(): return lax.ppermute(a, axis, [(i, j % n) for i, j in pairs])  16.6 us
    all_to_all x1, blocking collectives, local(): lax.all_to_all(merged, ('y', 'core'), split_axis=0, concat_axis=1, tiled=...  12.1 us
    pallas_call x4, Pallas kernels, attn(): pl.pallas_call(functools.partial(attn_kernel, deltas, blocks, bool(before...  10.5 us
  transfers between devices with their start and end apart: 9, of which 6 were waited for; matrix products, arithmetic and copies ran while one was open for 2% of the time, Pallas kernels for 16%

profile of v1, /device:TPU:36, one launch (start us, length us, event | category | flops | bytes accessed | tf_op | source)
XLA Modules:
  0.0 59.8 jit_solution(10219373476224067773)
XLA Ops:
  0.0 0.9 %shard_map.46 = (bf16[520,128]{1,0:T(8,128)(2,1)S(1)}, bf16[8,128]{1,0:T(8,128)(2,1)S(1)}) custom-call(bf16[256,128]{1,0:T(8,128)(2,1)} %bitcast.13, bf16[256,128]{1,0:T(8,128)(2,1)} %bitcast.14, s32[2,128]{1,0:T(2,128)} %bitcast.15), custom_call_target="tpu_custom_call" | custom-call | tf_op jit(solution)/shard_map/pallas_call | solution.py:55
  0.9 5.5 %collective-permute-start.1 = (bf16[520,128]{1,0:T(8,128)(2,1)S(1)}, bf16[520,128]{1,0:T(8,128)(2,1)S(1)}, u32[]{:S(2)}, u32[]{:S(2)}) collective-permute-start(bf16[520,128]{1,0:T(8,128)(2,1)S(1)} %get-tuple-element.15.refs_0_), channel_id=1, source_target_pairs={{0,48},{8,56},{16,0},{24,8},{32,16},{40,24},{48,32},{56,40},{1,49}... | collective-permute-start | bytes 399368 | tf_op jit(solution)/shard_map/ppermute | solution.py:258
  6.4 0.0 collective-permute-start
  6.4 1.0 %copy.5 = bf16[4,256,128]{2,1,0:T(8,128)(2,1)S(1)} copy(bf16[4,256,128]{2,0,1:T(4,128)(2,1)} %bitcast.12) | data formatting | bytes 524288 | tf_op jit(solution)/shard_map/transpose | solution.py:263
  7.4 2.4 %collective-permute-start.6 = (bf16[1032,128]{1,0:T(8,128)(2,1)S(1)}, bf16[1032,128]{1,0:T(8,128)(2,1)S(1)}, u32[]{:S(2)}, u32[]{:S(2)}) collective-permute-start(bf16[1032,128]{1,0:T(8,128)(2,1)S(1)} %pad_maximum_fusion.2.refs_6_), channel_id=1, source_target_pairs={{128,0},{192,64},{129,1},{193,65},{130,2},{194,66},{131,3},{195,67... | collective-permute-start | bytes 792584 | tf_op jit(solution)/shard_map/ppermute | solution.py:258
  9.9 1.9 %collective-permute-start.5 = (bf16[1032,128]{1,0:T(8,128)(2,1)S(1)}, bf16[1032,128]{1,0:T(8,128)(2,1)S(1)}, u32[]{:S(2)}, u32[]{:S(2)}) collective-permute-start(bf16[1032,128]{1,0:T(8,128)(2,1)S(1)} %pad_maximum_fusion.2.refs_6_), channel_id=1, source_target_pairs={{64,0},{128,64},{192,128},{65,1},{129,65},{193,129},{66,2},{130,66... | collective-permute-start | bytes 792584 | tf_op jit(solution)/shard_map/ppermute | solution.py:258
  11.8 0.0 collective-permute-done.1.refs_2_
  11.8 4.6 %collective-permute-done.refs_1_ = bf16[520,128]{1,0:T(8,128)(2,1)S(1)} collective-permute-done((bf16[520,128]{1,0:T(8,128)(2,1)S(1)}, bf16[520,128]{1,0:T(8,128)(2,1)S(1)}, u32[]{:S(2)}, u32[]{:S(2)}) %collective-permute-start) | collective-permute-done | bytes 133152 | tf_op jit(solution)/shard_map/ppermute | solution.py:258
  16.4 0.6 %collective-permute-start.4 = (bf16[1040,128]{1,0:T(8,128)(2,1)S(1)}, bf16[1040,128]{1,0:T(8,128)(2,1)S(1)}, u32[]{:S(2)}, u32[]{:S(2)}) collective-permute-start(bf16[1040,128]{1,0:T(8,128)(2,1)S(1)} %get-tuple-element.25), channel_id=1, source_target_pairs={{0,56},{8,0},{16,8},{24,16},{32,24},{40,32},{48,40},{56,48},{1,57}... | collective-permute-start | bytes 798728 | tf_op jit(solution)/shard_map/ppermute | solution.py:258
  17.0 1.5 %collective-permute-start.3 = (bf16[1040,128]{1,0:T(8,128)(2,1)S(1)}, bf16[1040,128]{1,0:T(8,128)(2,1)S(1)}, u32[]{:S(2)}, u32[]{:S(2)}) collective-permute-start(bf16[1040,128]{1,0:T(8,128)(2,1)S(1)} %get-tuple-element.26), channel_id=1, source_target_pairs={{0,8},{8,16},{16,24},{24,32},{32,40},{40,48},{48,56},{56,0},{1,9},... | collective-permute-start | bytes 798728 | tf_op jit(solution)/shard_map/ppermute | solution.py:258
  18.5 1.4 %collective-permute-start.2 = (bf16[520,128]{1,0:T(8,128)(2,1)S(1)}, bf16[520,128]{1,0:T(8,128)(2,1)S(1)}, u32[]{:S(2)}, u32[]{:S(2)}) collective-permute-start(bf16[520,128]{1,0:T(8,128)(2,1)S(1)} %get-tuple-element.15.refs_0_), channel_id=1, source_target_pairs={{0,32},{8,40},{16,48},{24,56},{32,0},{40,8},{48,16},{56,24},{1,33}... | collective-permute-start | bytes 399368 | tf_op jit(solution)/shard_map/ppermute | solution.py:258
  19.9 0.0 collective-permute-done.6.refs_4_.refs_3_
  20.0 3.5 %collective-permute-done.5.refs_3_ = bf16[1032,128]{1,0:T(8,128)(2,1)S(1)} collective-permute-done((bf16[1032,128]{1,0:T(8,128)(2,1)S(1)}, bf16[1032,128]{1,0:T(8,128)(2,1)S(1)}, u32[]{:S(2)}, u32[]{:S(2)}) %collective-permute-start.5) | collective-permute-done | bytes 264224 | tf_op jit(solution)/shard_map/ppermute | solution.py:258
  23.4 3.0 %shard_map.48 = (f32[1024,128]{1,0:T(8,128)S(1)}, f32[1024,128]{1,0:T(8,128)S(1)}, f32[1024,128]{1,0:T(8,128)S(1)}, f32[1024,128]{1,0:T(8,128)S(1)}, f32[1024,128]{1,0:T(8,128)S(1)}, /*index=5*/f32[1024,128]{1,0:T(8,128)S(1)}) custom-call(bf16[520,128]{1,0:T(8,128)(2,1)S(1)} %get-tuple-element.15.refs_0_, bf16[520,128]{1,0:T(8,128)(2,1)S(1)} %collective-permute-done.refs_1_, ...), custom_call_target="tpu_custom_call" | custom-call | flops 805306368 | bytes 1048576 | tf_op jit(solution)/shard_map/pallas_call | solution.py:194
  26.4 3.2 %collective-permute-done.2.refs_3_.refs_0_ = bf16[520,128]{1,0:T(8,128)(2,1)S(1)} collective-permute-done((bf16[520,128]{1,0:T(8,128)(2,1)S(1)}, bf16[520,128]{1,0:T(8,128)(2,1)S(1)}, u32[]{:S(2)}, u32[]{:S(2)}) %collective-permute-start.2) | collective-permute-done | bytes 133152 | tf_op jit(solution)/shard_map/ppermute | solution.py:258
  29.6 0.2 collective-permute-done.4.refs_5_.refs_2_
  29.8 0.0 collective-permute-done.3.refs_4_.refs_1_
  29.8 1.0 %shard_map.50 = bf16[1048,128]{1,0:T(8,128)(2,1)S(1)} custom-call(bf16[520,128]{1,0:T(8,128)(2,1)S(1)} %collective-permute-done.2.refs_3_.refs_0_, bf16[1040,128]{1,0:T(8,128)(2,1)S(1)} %collective-permute-done.3.refs_4_.refs_1_, bf16[1040,128]{1,0:T(8,128)(2,1)S(1)} %collective-permute-done.4.refs_5_.refs_2_, ...), custom_call_target="tpu_custom_call" | custom-call | flops 671088640 | bytes 1048576 | tf_op jit(solution)/shard_map/pallas_call | solution.py:194
  30.8 1.3 %collective-permute-start.8 = (bf16[1048,128]{1,0:T(8,128)(2,1)S(1)}, bf16[1048,128]{1,0:T(8,128)(2,1)S(1)}, u32[]{:S(2)}, u32[]{:S(2)}) collective-permute-start(bf16[1048,128]{1,0:T(8,128)(2,1)S(1)} %shard_map.50), channel_id=1, source_target_pairs={{0,128},{64,192},{1,129},{65,193},{2,130},{66,194},{3,131},{67,195... | collective-permute-start | bytes 804872 | tf_op jit(solution)/shard_map/ppermute | solution.py:258
  32.1 4.0 %shard_map.49 = bf16[1048,128]{1,0:T(8,128)(2,1)S(1)} custom-call(bf16[520,128]{1,0:T(8,128)(2,1)S(1)} %collective-permute-done.2.refs_3_.refs_0_, bf16[1040,128]{1,0:T(8,128)(2,1)S(1)} %collective-permute-done.3.refs_4_.refs_1_, bf16[1040,128]{1,0:T(8,128)(2,1)S(1)} %collective-permute-done.4.refs_5_.refs_2_, ...), custom_call_target="tpu_custom_call" | custom-call | flops 671088640 | bytes 1048576 | tf_op jit(solution)/shard_map/pallas_call | solution.py:194
  36.1 1.9 %collective-permute-start.7 = (bf16[1048,128]{1,0:T(8,128)(2,1)S(1)}, bf16[1048,128]{1,0:T(8,128)(2,1)S(1)}, u32[]{:S(2)}, u32[]{:S(2)}) collective-permute-start(bf16[1048,128]{1,0:T(8,128)(2,1)S(1)} %shard_map.49), channel_id=1, source_target_pairs={{0,64},{64,128},{128,192},{1,65},{65,129},{129,193},{2,66},{66,130... | collective-permute-start | bytes 804872 | tf_op jit(solution)/shard_map/ppermute | solution.py:258
  38.0 2.5 %shard_map.47 = (f32[1024,128]{1,0:T(8,128)S(1)}, f32[8,128]{1,0:T(8,128)S(1)}) custom-call(bf16[520,128]{1,0:T(8,128)(2,1)S(1)} %get-tuple-element.15.refs_0_, bf16[520,128]{1,0:T(8,128)(2,1)S(1)} %collective-permute-done.refs_1_, bf16[520,128]{1,0:T(8,128)(2,1)S(1)} %collective-permute-done.1.refs_2_, ...), custom_call_target="tpu_custom_call" | custom-call | flops 1073741824 | bytes 1048576 | tf_op jit(solution)/shard_map/pallas_call | solution.py:194
  40.5 2.4 %collective-permute-done.8.c_ref = bf16[1048,128]{1,0:T(8,128)(2,1)S(1)} collective-permute-done((bf16[1048,128]{1,0:T(8,128)(2,1)S(1)}, bf16[1048,128]{1,0:T(8,128)(2,1)S(1)}, u32[]{:S(2)}, u32[]{:S(2)}) %collective-permute-start.8) | collective-permute-done | bytes 268320 | tf_op jit(solution)/shard_map/ppermute | solution.py:258
  43.0 3.4 %collective-permute-done.7.b_ref = bf16[1048,128]{1,0:T(8,128)(2,1)S(1)} collective-permute-done((bf16[1048,128]{1,0:T(8,128)(2,1)S(1)}, bf16[1048,128]{1,0:T(8,128)(2,1)S(1)}, u32[]{:S(2)}, u32[]{:S(2)}) %collective-permute-start.7) | collective-permute-done | bytes 268320 | tf_op jit(solution)/shard_map/ppermute | solution.py:258
  46.3 0.7 %shard_map.51 = bf16[256,512]{1,0:T(8,128)(2,1)S(1)} custom-call(f32[1024,128]{1,0:T(8,128)S(1)} %get-tuple-element.17.a_ref, f32[8,128]{1,0:T(8,128)S(1)} %get-tuple-element.18.lse_ref, bf16[1048,128]{1,0:T(8,128)(2,1)S(1)} %collective-permute-done.7.b_ref, bf16[1048,128]{1,0:T(8,128)(2,1)S(1)} %collective-permute-done.8.c_ref), custom_call_target="tpu_custom_call" | custom-call | tf_op jit(solution)/shard_map/pallas_call | solution.py:245
  47.0 12.1 %all_to_all.19 = bf16[8,32,512]{2,1,0:T(8,128)(2,1)S(1)} all-to-all(bf16[8,32,512]{2,1,0:T(8,128)(2,1)S(1)} %bitcast.9), channel_id=1, replica_groups=mesh['x'=4,'z'=8,'y'=4,'core'=2] {'y','core'}, dimensions={0} | all-to-all | bytes 524288 | tf_op jit(solution)/shard_map/all_to_all | solution.py:281
  59.1 0.7 %copy.7 = bf16[8,4,8,512]{3,2,0,1:T(8,128)(2,1)} copy(bf16[8,4,8,512]{3,2,1,0:T(8,128)(2,1)S(1)} %bitcast.11) | data formatting | bytes 524288 | tf_op jit(solution)/shard_map/all_to_all | solution.py:281
  (2 shorter events, 0.1 us)
Async XLA Ops:
  0.9 10.9 %collective-permute-start.1 = (bf16[520,128]{1,0:T(8,128)(2,1)S(1)}, bf16[520,128]{1,0:T(8,128)(2,1)S(1)}, u32[]{:S(2)}, u32[]{:S(2)}) collective-permute-start(bf16[520,128]{1,0:T(8,128)(2,1)S(1)} %get-tuple-element.15.refs_0_), channel_id=1, source_target_pairs={{0,48},{8,56},{16,0},{24,8},{32,16},{40,24},{48,32},{56,40},{1,49}... | collective-permute-start | bytes 399368 | tf_op jit(solution)/shard_map/ppermute | solution.py:258
  6.4 10.0 %collective-permute-start = (bf16[520,128]{1,0:T(8,128)(2,1)S(1)}, bf16[520,128]{1,0:T(8,128)(2,1)S(1)}, u32[]{:S(2)}, u32[]{:S(2)}) collective-permute-start(bf16[520,128]{1,0:T(8,128)(2,1)S(1)} %get-tuple-element.15.refs_0_), channel_id=1, source_target_pairs={{0,16},{8,24},{16,32},{24,40},{32,48},{40,56},{48,0},{56,8},{1,17}... | collective-permute-start | bytes 399368 | tf_op jit(solution)/shard_map/ppermute | solution.py:258
  7.4 12.5 %collective-permute-start.6 = (bf16[1032,128]{1,0:T(8,128)(2,1)S(1)}, bf16[1032,128]{1,0:T(8,128)(2,1)S(1)}, u32[]{:S(2)}, u32[]{:S(2)}) collective-permute-start(bf16[1032,128]{1,0:T(8,128)(2,1)S(1)} %pad_maximum_fusion.2.refs_6_), channel_id=1, source_target_pairs={{128,0},{192,64},{129,1},{193,65},{130,2},{194,66},{131,3},{195,67... | collective-permute-start | bytes 792584 | tf_op jit(solution)/shard_map/ppermute | solution.py:258
  9.9 13.6 %collective-permute-start.5 = (bf16[1032,128]{1,0:T(8,128)(2,1)S(1)}, bf16[1032,128]{1,0:T(8,128)(2,1)S(1)}, u32[]{:S(2)}, u32[]{:S(2)}) collective-permute-start(bf16[1032,128]{1,0:T(8,128)(2,1)S(1)} %pad_maximum_fusion.2.refs_6_), channel_id=1, source_target_pairs={{64,0},{128,64},{192,128},{65,1},{129,65},{193,129},{66,2},{130,66... | collective-permute-start | bytes 792584 | tf_op jit(solution)/shard_map/ppermute | solution.py:258
  16.4 13.4 %collective-permute-start.4 = (bf16[1040,128]{1,0:T(8,128)(2,1)S(1)}, bf16[1040,128]{1,0:T(8,128)(2,1)S(1)}, u32[]{:S(2)}, u32[]{:S(2)}) collective-permute-start(bf16[1040,128]{1,0:T(8,128)(2,1)S(1)} %get-tuple-element.25), channel_id=1, source_target_pairs={{0,56},{8,0},{16,8},{24,16},{32,24},{40,32},{48,40},{56,48},{1,57}... | collective-permute-start | bytes 798728 | tf_op jit(solution)/shard_map/ppermute | solution.py:258
  17.0 12.8 %collective-permute-start.3 = (bf16[1040,128]{1,0:T(8,128)(2,1)S(1)}, bf16[1040,128]{1,0:T(8,128)(2,1)S(1)}, u32[]{:S(2)}, u32[]{:S(2)}) collective-permute-start(bf16[1040,128]{1,0:T(8,128)(2,1)S(1)} %get-tuple-element.26), channel_id=1, source_target_pairs={{0,8},{8,16},{16,24},{24,32},{32,40},{40,48},{48,56},{56,0},{1,9},... | collective-permute-start | bytes 798728 | tf_op jit(solution)/shard_map/ppermute | solution.py:258
  18.5 11.1 %collective-permute-start.2 = (bf16[520,128]{1,0:T(8,128)(2,1)S(1)}, bf16[520,128]{1,0:T(8,128)(2,1)S(1)}, u32[]{:S(2)}, u32[]{:S(2)}) collective-permute-start(bf16[520,128]{1,0:T(8,128)(2,1)S(1)} %get-tuple-element.15.refs_0_), channel_id=1, source_target_pairs={{0,32},{8,40},{16,48},{24,56},{32,0},{40,8},{48,16},{56,24},{1,33}... | collective-permute-start | bytes 399368 | tf_op jit(solution)/shard_map/ppermute | solution.py:258
  30.8 12.2 %collective-permute-start.8 = (bf16[1048,128]{1,0:T(8,128)(2,1)S(1)}, bf16[1048,128]{1,0:T(8,128)(2,1)S(1)}, u32[]{:S(2)}, u32[]{:S(2)}) collective-permute-start(bf16[1048,128]{1,0:T(8,128)(2,1)S(1)} %shard_map.50), channel_id=1, source_target_pairs={{0,128},{64,192},{1,129},{65,193},{2,130},{66,194},{3,131},{67,195... | collective-permute-start | bytes 804872 | tf_op jit(solution)/shard_map/ppermute | solution.py:258
  36.1 10.2 %collective-permute-start.7 = (bf16[1048,128]{1,0:T(8,128)(2,1)S(1)}, bf16[1048,128]{1,0:T(8,128)(2,1)S(1)}, u32[]{:S(2)}, u32[]{:S(2)}) collective-permute-start(bf16[1048,128]{1,0:T(8,128)(2,1)S(1)} %shard_map.49), channel_id=1, source_target_pairs={{0,64},{64,128},{128,192},{1,65},{65,129},{129,193},{2,66},{66,130... | collective-permute-start | bytes 804872 | tf_op jit(solution)/shard_map/ppermute | solution.py:258

commit v2 on v1

--- a/solution.py
+++ b/solution.py
@@ -267,14 +267,15 @@
     dn2 = along(kv, "z", -2, NZ)
     q2 = along(q, "x", -2, NX)
     q1 = along(q, "x", -1, NX)
-    far = along(kv, "z", 4, NZ)
     up13 = along(jnp.concatenate([kv, up2], axis=0), "z", 1, NZ)
     dn13 = along(jnp.concatenate([kv, dn2], axis=0), "z", -1, NZ)
+    far = along(up2, "z", 2, NZ)
     first, rest = [kv, up2, dn2], [far, up13, dn13]
-    near = attn((1, 2), NEAR, first, [q1, q2], (), "state")
-    (o1,) = attn((1,), REST, rest, [q1], near[:3], "send")
+    near1 = attn((1,), NEAR, first, [q1], (), "state")
+    near2 = attn((2,), NEAR, first, [q2], (), "state")
+    (o1,) = attn((1,), REST, rest, [q1], near1, "send")
     r1 = along(o1, "x", 1, NX)
-    (o2,) = attn((2,), REST, rest, [q2], near[3:], "send")
+    (o2,) = attn((2,), REST, rest, [q2], near2, "send")
     r2 = along(o2, "x", 2, NX)
     o0, lse0 = attn((0,), EVERY, first + rest, [q], (), "keep")
     merged = combine(o0, lse0, r1, r2)

time: 60.1 us -> 60.1 us (level)
  starting transfers between devices: 16.6 us -> 19.8 us
  waiting for transfers between devices: 17.3 us -> 14.3 us
    ppermute x9, starting transfers between devices: 16.6 us -> 19.8 us  [along(): return lax.ppermute(a, axis, [(i, j % n) for i, j in pairs])]
    ppermute x9, waiting for transfers between devices: 17.3 us -> 14.3 us  [along(): return lax.ppermute(a, axis, [(i, j % n) for i, j in pairs])]
    pallas_call x4 -> x5, Pallas kernels: 10.5 us -> 10.6 us  [attn(): pl.pallas_call(functools.partial(attn_kernel, deltas, blocks, bool(before...]
  transfers between devices with their start and end apart: 9 -> 9, of which waited for: 6 -> 5; matrix products, arithmetic and copies ran while one was open for 2% -> 2% of each run, Pallas kernels for 16% -> 16%
where the time goes in v2:
time: 60.1 us; the launch traced here: 59.8 us
  starting transfers between devices  19.8 us (33%)
  waiting for transfers between devices  14.3 us (24%)
  Pallas kernels  12.1 us (20%)
  blocking collectives  11.8 us (20%)
  local copies, waits for them, and re-layouts  1.71 us (3%)
    ppermute x9, starting transfers between devices, along(): return lax.ppermute(a, axis, [(i, j % n) for i, j in pairs])  19.8 us
    ppermute x9, waiting for transfers between devices, along(): return lax.ppermute(a, axis, [(i, j % n) for i, j in pairs])  14.3 us
    all_to_all x1, blocking collectives, local(): lax.all_to_all(merged, ('y', 'core'), split_axis=0, concat_axis=1, tiled=...  11.8 us
    pallas_call x5, Pallas kernels, attn(): pl.pallas_call(functools.partial(attn_kernel, deltas, blocks, bool(before...  10.6 us
  transfers between devices with their start and end apart: 9, of which 5 were waited for; matrix products, arithmetic and copies ran while one was open for 2% of the time, Pallas kernels for 16%

profile of v2, /device:TPU:36, one launch (start us, length us, event | category | flops | bytes accessed | tf_op | source)
XLA Modules:
  0.0 59.8 jit_solution(2498077095255552942)
XLA Ops:
  0.0 0.9 %shard_map.46 = (bf16[520,128]{1,0:T(8,128)(2,1)S(1)}, bf16[8,128]{1,0:T(8,128)(2,1)S(1)}) custom-call(bf16[256,128]{1,0:T(8,128)(2,1)} %bitcast.13, bf16[256,128]{1,0:T(8,128)(2,1)} %bitcast.14, s32[2,128]{1,0:T(2,128)} %bitcast.15), custom_call_target="tpu_custom_call" | custom-call | tf_op jit(solution)/shard_map/pallas_call | solution.py:55
  0.9 3.3 %collective-permute-start = (bf16[520,128]{1,0:T(8,128)(2,1)S(1)}, bf16[520,128]{1,0:T(8,128)(2,1)S(1)}, u32[]{:S(2)}, u32[]{:S(2)}) collective-permute-start(bf16[520,128]{1,0:T(8,128)(2,1)S(1)} %get-tuple-element.15.refs_0_), channel_id=1, source_target_pairs={{0,16},{8,24},{16,32},{24,40},{32,48},{40,56},{48,0},{56,8},{1,17}... | collective-permute-start | bytes 399368 | tf_op jit(solution)/shard_map/ppermute | solution.py:258
  4.3 2.2 %collective-permute-start.1 = (bf16[520,128]{1,0:T(8,128)(2,1)S(1)}, bf16[520,128]{1,0:T(8,128)(2,1)S(1)}, u32[]{:S(2)}, u32[]{:S(2)}) collective-permute-start(bf16[520,128]{1,0:T(8,128)(2,1)S(1)} %get-tuple-element.15.refs_0_), channel_id=1, source_target_pairs={{0,48},{8,56},{16,0},{24,8},{32,16},{40,24},{48,32},{56,40},{1,49}... | collective-permute-start | bytes 399368 | tf_op jit(solution)/shard_map/ppermute | solution.py:258
  6.5 1.0 %copy.5 = bf16[4,256,128]{2,1,0:T(8,128)(2,1)S(1)} copy(bf16[4,256,128]{2,0,1:T(4,128)(2,1)} %bitcast.12) | data formatting | bytes 524288 | tf_op jit(solution)/shard_map/transpose | solution.py:263
  7.5 2.4 %collective-permute-start.7 = (bf16[1032,128]{1,0:T(8,128)(2,1)S(1)}, bf16[1032,128]{1,0:T(8,128)(2,1)S(1)}, u32[]{:S(2)}, u32[]{:S(2)}) collective-permute-start(bf16[1032,128]{1,0:T(8,128)(2,1)S(1)} %pad_maximum_fusion.2.refs_6_), channel_id=1, source_target_pairs={{128,0},{192,64},{129,1},{193,65},{130,2},{194,66},{131,3},{195,67... | collective-permute-start | bytes 792584 | tf_op jit(solution)/shard_map/ppermute | solution.py:258
  9.9 1.9 %collective-permute-start.5 = (bf16[1032,128]{1,0:T(8,128)(2,1)S(1)}, bf16[1032,128]{1,0:T(8,128)(2,1)S(1)}, u32[]{:S(2)}, u32[]{:S(2)}) collective-permute-start(bf16[1032,128]{1,0:T(8,128)(2,1)S(1)} %pad_maximum_fusion.2.refs_6_), channel_id=1, source_target_pairs={{64,0},{128,64},{192,128},{65,1},{129,65},{193,129},{66,2},{130,66... | collective-permute-start | bytes 792584 | tf_op jit(solution)/shard_map/ppermute | solution.py:258
  11.9 0.9 %collective-permute-done.refs_1_ = bf16[520,128]{1,0:T(8,128)(2,1)S(1)} collective-permute-done((bf16[520,128]{1,0:T(8,128)(2,1)S(1)}, bf16[520,128]{1,0:T(8,128)(2,1)S(1)}, u32[]{:S(2)}, u32[]{:S(2)}) %collective-permute-start) | collective-permute-done | bytes 133152 | tf_op jit(solution)/shard_map/ppermute | solution.py:258
  12.8 0.0 collective-permute-done.1.refs_2_
  12.8 4.6 %collective-permute-start.3 = (bf16[1040,128]{1,0:T(8,128)(2,1)S(1)}, bf16[1040,128]{1,0:T(8,128)(2,1)S(1)}, u32[]{:S(2)}, u32[]{:S(2)}) collective-permute-start(bf16[1040,128]{1,0:T(8,128)(2,1)S(1)} %get-tuple-element.26), channel_id=1, source_target_pairs={{0,8},{8,16},{16,24},{24,32},{32,40},{40,48},{48,56},{56,0},{1,9},... | collective-permute-start | bytes 798728 | tf_op jit(solution)/shard_map/ppermute | solution.py:258
  17.4 0.0 collective-permute-start.4
  17.4 2.1 %collective-permute-start.2 = (bf16[520,128]{1,0:T(8,128)(2,1)S(1)}, bf16[520,128]{1,0:T(8,128)(2,1)S(1)}, u32[]{:S(2)}, u32[]{:S(2)}) collective-permute-start(bf16[520,128]{1,0:T(8,128)(2,1)S(1)} %collective-permute-done.refs_1_), channel_id=1, source_target_pairs={{0,16},{8,24},{16,32},{24,40},{32,48},{40,56},{48,0},{56,8},{1,17}... | collective-permute-start | bytes 399368 | tf_op jit(solution)/shard_map/ppermute | solution.py:258
  19.5 0.0 collective-permute-done.7.refs_3_
  19.5 0.6 %shard_map.50 = (f32[1024,128]{1,0:T(8,128)S(1)}, f32[1024,128]{1,0:T(8,128)S(1)}, f32[1024,128]{1,0:T(8,128)S(1)}) custom-call(bf16[520,128]{1,0:T(8,128)(2,1)S(1)} %get-tuple-element.15.refs_0_, bf16[520,128]{1,0:T(8,128)(2,1)S(1)} %collective-permute-done.refs_1_, bf16[520,128]{1,0:T(8,128)(2,1)S(1)} %collective-permute-done.1.refs_2_, ...), custom_call_target="tpu_custom_call" | custom-call | flops 402653184 | bytes 1048576 | tf_op jit(solution)/shard_map/pallas_call | solution.py:194
  20.1 3.4 %collective-permute-done.5.refs_3_ = bf16[1032,128]{1,0:T(8,128)(2,1)S(1)} collective-permute-done((bf16[1032,128]{1,0:T(8,128)(2,1)S(1)}, bf16[1032,128]{1,0:T(8,128)(2,1)S(1)}, u32[]{:S(2)}, u32[]{:S(2)}) %collective-permute-start.5) | collective-permute-done | bytes 264224 | tf_op jit(solution)/shard_map/ppermute | solution.py:258
  23.5 2.4 %shard_map.48 = (f32[1024,128]{1,0:T(8,128)S(1)}, f32[1024,128]{1,0:T(8,128)S(1)}, f32[1024,128]{1,0:T(8,128)S(1)}) custom-call(bf16[520,128]{1,0:T(8,128)(2,1)S(1)} %get-tuple-element.15.refs_0_, bf16[520,128]{1,0:T(8,128)(2,1)S(1)} %collective-permute-done.refs_1_, bf16[520,128]{1,0:T(8,128)(2,1)S(1)} %collective-permute-done.1.refs_2_, ...), custom_call_target="tpu_custom_call" | custom-call | flops 402653184 | bytes 1048576 | tf_op jit(solution)/shard_map/pallas_call | solution.py:194
  25.9 3.4 %collective-permute-done.2.refs_3_.refs_0_ = bf16[520,128]{1,0:T(8,128)(2,1)S(1)} collective-permute-done((bf16[520,128]{1,0:T(8,128)(2,1)S(1)}, bf16[520,128]{1,0:T(8,128)(2,1)S(1)}, u32[]{:S(2)}, u32[]{:S(2)}) %collective-permute-start.2) | collective-permute-done | bytes 133152 | tf_op jit(solution)/shard_map/ppermute | solution.py:258
  29.3 0.0 collective-permute-done.3.refs_4_.refs_1_
  29.3 0.0 collective-permute-done.4.refs_5_.refs_2_
  29.3 1.0 %shard_map.51 = bf16[1048,128]{1,0:T(8,128)(2,1)S(1)} custom-call(bf16[520,128]{1,0:T(8,128)(2,1)S(1)} %collective-permute-done.2.refs_3_.refs_0_, bf16[1040,128]{1,0:T(8,128)(2,1)S(1)} %collective-permute-done.3.refs_4_.refs_1_, bf16[1040,128]{1,0:T(8,128)(2,1)S(1)} %collective-permute-done.4.refs_5_.refs_2_, ...), custom_call_target="tpu_custom_call" | custom-call | flops 671088640 | bytes 1048576 | tf_op jit(solution)/shard_map/pallas_call | solution.py:194
  30.3 1.3 %collective-permute-start.8 = (bf16[1048,128]{1,0:T(8,128)(2,1)S(1)}, bf16[1048,128]{1,0:T(8,128)(2,1)S(1)}, u32[]{:S(2)}, u32[]{:S(2)}) collective-permute-start(bf16[1048,128]{1,0:T(8,128)(2,1)S(1)} %shard_map.51), channel_id=1, source_target_pairs={{0,128},{64,192},{1,129},{65,193},{2,130},{66,194},{3,131},{67,195... | collective-permute-start | bytes 804872 | tf_op jit(solution)/shard_map/ppermute | solution.py:258
  31.6 4.0 %shard_map.49 = bf16[1048,128]{1,0:T(8,128)(2,1)S(1)} custom-call(bf16[520,128]{1,0:T(8,128)(2,1)S(1)} %collective-permute-done.2.refs_3_.refs_0_, bf16[1040,128]{1,0:T(8,128)(2,1)S(1)} %collective-permute-done.3.refs_4_.refs_1_, bf16[1040,128]{1,0:T(8,128)(2,1)S(1)} %collective-permute-done.4.refs_5_.refs_2_, ...), custom_call_target="tpu_custom_call" | custom-call | flops 671088640 | bytes 1048576 | tf_op jit(solution)/shard_map/pallas_call | solution.py:194
  35.6 1.9 %collective-permute-start.6 = (bf16[1048,128]{1,0:T(8,128)(2,1)S(1)}, bf16[1048,128]{1,0:T(8,128)(2,1)S(1)}, u32[]{:S(2)}, u32[]{:S(2)}) collective-permute-start(bf16[1048,128]{1,0:T(8,128)(2,1)S(1)} %shard_map.49), channel_id=1, source_target_pairs={{0,64},{64,128},{128,192},{1,65},{65,129},{129,193},{2,66},{66,130... | collective-permute-start | bytes 804872 | tf_op jit(solution)/shard_map/ppermute | solution.py:258
  37.6 2.5 %shard_map.47 = (f32[1024,128]{1,0:T(8,128)S(1)}, f32[8,128]{1,0:T(8,128)S(1)}) custom-call(bf16[520,128]{1,0:T(8,128)(2,1)S(1)} %get-tuple-element.15.refs_0_, bf16[520,128]{1,0:T(8,128)(2,1)S(1)} %collective-permute-done.refs_1_, bf16[520,128]{1,0:T(8,128)(2,1)S(1)} %collective-permute-done.1.refs_2_, ...), custom_call_target="tpu_custom_call" | custom-call | flops 1073741824 | bytes 1048576 | tf_op jit(solution)/shard_map/pallas_call | solution.py:194
  40.0 3.0 %collective-permute-done.8.c_ref = bf16[1048,128]{1,0:T(8,128)(2,1)S(1)} collective-permute-done((bf16[1048,128]{1,0:T(8,128)(2,1)S(1)}, bf16[1048,128]{1,0:T(8,128)(2,1)S(1)}, u32[]{:S(2)}, u32[]{:S(2)}) %collective-permute-start.8) | collective-permute-done | bytes 268320 | tf_op jit(solution)/shard_map/ppermute | solution.py:258
  43.0 3.6 %collective-permute-done.6.b_ref = bf16[1048,128]{1,0:T(8,128)(2,1)S(1)} collective-permute-done((bf16[1048,128]{1,0:T(8,128)(2,1)S(1)}, bf16[1048,128]{1,0:T(8,128)(2,1)S(1)}, u32[]{:S(2)}, u32[]{:S(2)}) %collective-permute-start.6) | collective-permute-done | bytes 268320 | tf_op jit(solution)/shard_map/ppermute | solution.py:258
  46.7 0.7 %shard_map.52 = bf16[256,512]{1,0:T(8,128)(2,1)S(1)} custom-call(f32[1024,128]{1,0:T(8,128)S(1)} %get-tuple-element.17.a_ref, f32[8,128]{1,0:T(8,128)S(1)} %get-tuple-element.18.lse_ref, bf16[1048,128]{1,0:T(8,128)(2,1)S(1)} %collective-permute-done.6.b_ref, bf16[1048,128]{1,0:T(8,128)(2,1)S(1)} %collective-permute-done.8.c_ref), custom_call_target="tpu_custom_call" | custom-call | tf_op jit(solution)/shard_map/pallas_call | solution.py:245
  47.3 11.8 %all_to_all.19 = bf16[8,32,512]{2,1,0:T(8,128)(2,1)S(1)} all-to-all(bf16[8,32,512]{2,1,0:T(8,128)(2,1)S(1)} %bitcast.9), channel_id=1, replica_groups=mesh['x'=4,'z'=8,'y'=4,'core'=2] {'y','core'}, dimensions={0} | all-to-all | bytes 524288 | tf_op jit(solution)/shard_map/all_to_all | solution.py:282
  59.1 0.7 %copy.7 = bf16[8,4,8,512]{3,2,0,1:T(8,128)(2,1)} copy(bf16[8,4,8,512]{3,2,1,0:T(8,128)(2,1)S(1)} %bitcast.11) | data formatting | bytes 524288 | tf_op jit(solution)/shard_map/all_to_all | solution.py:282
  (2 shorter events, 0.1 us)
Async XLA Ops:
  0.9 11.9 %collective-permute-start = (bf16[520,128]{1,0:T(8,128)(2,1)S(1)}, bf16[520,128]{1,0:T(8,128)(2,1)S(1)}, u32[]{:S(2)}, u32[]{:S(2)}) collective-permute-start(bf16[520,128]{1,0:T(8,128)(2,1)S(1)} %get-tuple-element.15.refs_0_), channel_id=1, source_target_pairs={{0,16},{8,24},{16,32},{24,40},{32,48},{40,56},{48,0},{56,8},{1,17}... | collective-permute-start | bytes 399368 | tf_op jit(solution)/shard_map/ppermute | solution.py:258
  4.3 8.5 %collective-permute-start.1 = (bf16[520,128]{1,0:T(8,128)(2,1)S(1)}, bf16[520,128]{1,0:T(8,128)(2,1)S(1)}, u32[]{:S(2)}, u32[]{:S(2)}) collective-permute-start(bf16[520,128]{1,0:T(8,128)(2,1)S(1)} %get-tuple-element.15.refs_0_), channel_id=1, source_target_pairs={{0,48},{8,56},{16,0},{24,8},{32,16},{40,24},{48,32},{56,40},{1,49}... | collective-permute-start | bytes 399368 | tf_op jit(solution)/shard_map/ppermute | solution.py:258
  7.5 12.0 %collective-permute-start.7 = (bf16[1032,128]{1,0:T(8,128)(2,1)S(1)}, bf16[1032,128]{1,0:T(8,128)(2,1)S(1)}, u32[]{:S(2)}, u32[]{:S(2)}) collective-permute-start(bf16[1032,128]{1,0:T(8,128)(2,1)S(1)} %pad_maximum_fusion.2.refs_6_), channel_id=1, source_target_pairs={{128,0},{192,64},{129,1},{193,65},{130,2},{194,66},{131,3},{195,67... | collective-permute-start | bytes 792584 | tf_op jit(solution)/shard_map/ppermute | solution.py:258
  9.9 13.6 %collective-permute-start.5 = (bf16[1032,128]{1,0:T(8,128)(2,1)S(1)}, bf16[1032,128]{1,0:T(8,128)(2,1)S(1)}, u32[]{:S(2)}, u32[]{:S(2)}) collective-permute-start(bf16[1032,128]{1,0:T(8,128)(2,1)S(1)} %pad_maximum_fusion.2.refs_6_), channel_id=1, source_target_pairs={{64,0},{128,64},{192,128},{65,1},{129,65},{193,129},{66,2},{130,66... | collective-permute-start | bytes 792584 | tf_op jit(solution)/shard_map/ppermute | solution.py:258
  12.8 16.5 %collective-permute-start.3 = (bf16[1040,128]{1,0:T(8,128)(2,1)S(1)}, bf16[1040,128]{1,0:T(8,128)(2,1)S(1)}, u32[]{:S(2)}, u32[]{:S(2)}) collective-permute-start(bf16[1040,128]{1,0:T(8,128)(2,1)S(1)} %get-tuple-element.26), channel_id=1, source_target_pairs={{0,8},{8,16},{16,24},{24,32},{32,40},{40,48},{48,56},{56,0},{1,9},... | collective-permute-start | bytes 798728 | tf_op jit(solution)/shard_map/ppermute | solution.py:258
  17.4 11.9 %collective-permute-start.4 = (bf16[1040,128]{1,0:T(8,128)(2,1)S(1)}, bf16[1040,128]{1,0:T(8,128)(2,1)S(1)}, u32[]{:S(2)}, u32[]{:S(2)}) collective-permute-start(bf16[1040,128]{1,0:T(8,128)(2,1)S(1)} %get-tuple-element.25), channel_id=1, source_target_pairs={{0,56},{8,0},{16,8},{24,16},{32,24},{40,32},{48,40},{56,48},{1,57}... | collective-permute-start | bytes 798728 | tf_op jit(solution)/shard_map/ppermute | solution.py:258
  17.4 11.9 %collective-permute-start.2 = (bf16[520,128]{1,0:T(8,128)(2,1)S(1)}, bf16[520,128]{1,0:T(8,128)(2,1)S(1)}, u32[]{:S(2)}, u32[]{:S(2)}) collective-permute-start(bf16[520,128]{1,0:T(8,128)(2,1)S(1)} %collective-permute-done.refs_1_), channel_id=1, source_target_pairs={{0,16},{8,24},{16,32},{24,40},{32,48},{40,56},{48,0},{56,8},{1,17}... | collective-permute-start | bytes 399368 | tf_op jit(solution)/shard_map/ppermute | solution.py:258
  30.3 12.7 %collective-permute-start.8 = (bf16[1048,128]{1,0:T(8,128)(2,1)S(1)}, bf16[1048,128]{1,0:T(8,128)(2,1)S(1)}, u32[]{:S(2)}, u32[]{:S(2)}) collective-permute-start(bf16[1048,128]{1,0:T(8,128)(2,1)S(1)} %shard_map.51), channel_id=1, source_target_pairs={{0,128},{64,192},{1,129},{65,193},{2,130},{66,194},{3,131},{67,195... | collective-permute-start | bytes 804872 | tf_op jit(solution)/shard_map/ppermute | solution.py:258
  35.6 11.0 %collective-permute-start.6 = (bf16[1048,128]{1,0:T(8,128)(2,1)S(1)}, bf16[1048,128]{1,0:T(8,128)(2,1)S(1)}, u32[]{:S(2)}, u32[]{:S(2)}) collective-permute-start(bf16[1048,128]{1,0:T(8,128)(2,1)S(1)} %shard_map.49), channel_id=1, source_target_pairs={{0,64},{64,128},{128,192},{1,65},{65,129},{129,193},{2,66},{66,130... | collective-permute-start | bytes 804872 | tf_op jit(solution)/shard_map/ppermute | solution.py:258

commit v3 on v2

--- a/solution.py
+++ b/solution.py
@@ -18,9 +18,15 @@
 HALF = 128
 NEG = -1e30
 PIECE = 2 * TOK + 8
-NEAR = ((0, 0, 0), (1, 0, 2), (2, 0, -2))
-REST = ((0, 0, 4), (1, 0, 1), (1, PIECE, 3), (2, 0, -1), (2, PIECE, -3))
-EVERY = NEAR + tuple((array + len(NEAR), row, shift) for array, row, shift in REST)
+NEAR = ((0, 0, 0, TOK, 0), (1, 0, 1, TOK, 2), (2, 0, 2, TOK, -2))
+REST = (
+    (0, 0, 0, TOK, 1),
+    (0, PIECE, 0, PIECE + TOK, 3),
+    (1, 0, 1, TOK, -1),
+    (1, PIECE, 1, PIECE + TOK, -3),
+    (2, 0, 3, 0, 4),
+)
+EVERY = NEAR + tuple((a + len(NEAR), i, b + len(NEAR), j, shift) for a, i, b, j, shift in REST)
 MIB = 1 << 20
 ROWS = TOK * HEADS
 GROUPS = ROWS // HALF
@@ -67,18 +73,17 @@
 
 def attn_kernel(deltas, blocks, merge, last, *refs):
     n, nb = len(deltas), len(blocks)
-    arrays = 1 + max(array for array, _, _ in blocks)
+    arrays = 1 + max(max(block[0], block[2]) for block in blocks)
     kv, refs = refs[:arrays], refs[arrays:]
     qs, refs = refs[:n], refs[n:]
     before, refs = (refs[: 3 * n], refs[3 * n :]) if merge else (None, refs)
     per = {"state": 3, "send": 1, "keep": 2}[last]
     outs, (kscr, vscr, sscr, acc, mscr, lscr, rows_scr, cscr) = refs[: per * n], refs[per * n :]
     x, z = lax.axis_index("x"), lax.axis_index("z")
-    for i, (array, row, shift) in enumerate(blocks):
-        ref = kv[array]
-        kscr[i] = ref[row : row + TOK, :]
-        vscr[i] = ref[row + TOK : row + 2 * TOK, :]
-        cnt = ref[row + 2 * TOK : row + PIECE, :].astype(jnp.float32)
+    for i, (k_at, k_row, v_at, v_row, shift) in enumerate(blocks):
+        kscr[i] = kv[k_at][k_row : k_row + TOK, :]
+        vscr[i] = kv[v_at][v_row : v_row + TOK, :]
+        cnt = kv[v_at][v_row + TOK : v_row + TOK + 8, :].astype(jnp.float32)
         cscr[i, 0] = lax.rem(z - shift + NZ, NZ)
         for d in (1, 2, 3):
             cscr[i, d] = jnp.max(cnt[d : d + 1, :]).astype(jnp.int32)
@@ -269,8 +274,9 @@
     q1 = along(q, "x", -1, NX)
     up13 = along(jnp.concatenate([kv, up2], axis=0), "z", 1, NZ)
     dn13 = along(jnp.concatenate([kv, dn2], axis=0), "z", -1, NZ)
-    far = along(up2, "z", 2, NZ)
-    first, rest = [kv, up2, dn2], [far, up13, dn13]
+    far_k = along(up2[0:TOK], "z", 2, NZ)
+    far_v = along(dn2[TOK:PIECE], "z", -2, NZ)
+    first, rest = [kv, up2, dn2], [up13, dn13, far_k, far_v]
     near1 = attn((1,), NEAR, first, [q1], (), "state")
     near2 = attn((2,), NEAR, first, [q2], (), "state")
     (o1,) = attn((1,), REST, rest, [q1], near1, "send")

time: 60.1 us -> 59 us (0.982)
  the two profiles are of different devices: /device:TPU:36 before, /device:TPU:4 now
where the time goes in v3:
time: 59 us; the launch traced here: 58.8 us
  starting transfers between devices  20.3 us (34%)
  waiting for transfers between devices  13.3 us (23%)
  blocking collectives  11.8 us (20%)
  Pallas kernels  11.5 us (19%)
  local copies, waits for them, and re-layouts  1.72 us (3%)
    ppermute x10, starting transfers between devices, along(): return lax.ppermute(a, axis, [(i, j % n) for i, j in pairs])  20.3 us
    ppermute x10, waiting for transfers between devices, along(): return lax.ppermute(a, axis, [(i, j % n) for i, j in pairs])  13.3 us
    all_to_all x1, blocking collectives, local(): lax.all_to_all(merged, ('y', 'core'), split_axis=0, concat_axis=1, tiled=...  11.8 us
    pallas_call x5, Pallas kernels, attn(): pl.pallas_call(functools.partial(attn_kernel, deltas, blocks, bool(before...  9.92 us
  transfers between devices with their start and end apart: 10, of which 5 were waited for; matrix products, arithmetic and copies ran while one was open for 2% of the time, Pallas kernels for 15%

profile of v3, /device:TPU:4, one launch (start us, length us, event | category | flops | bytes accessed | tf_op | source)
XLA Modules:
  0.0 58.8 jit_solution(8872515701908636550)
XLA Ops:
  0.0 0.9 %shard_map.46 = (bf16[520,128]{1,0:T(8,128)(2,1)S(1)}, bf16[8,128]{1,0:T(8,128)(2,1)S(1)}) custom-call(bf16[256,128]{1,0:T(8,128)(2,1)} %bitcast.13, bf16[256,128]{1,0:T(8,128)(2,1)} %bitcast.14, s32[2,128]{1,0:T(2,128)} %bitcast.15), custom_call_target="tpu_custom_call" | custom-call | tf_op jit(solution)/shard_map/pallas_call | solution.py:61
  0.9 3.3 %collective-permute-start = (bf16[520,128]{1,0:T(8,128)(2,1)S(1)}, bf16[520,128]{1,0:T(8,128)(2,1)S(1)}, u32[]{:S(2)}, u32[]{:S(2)}) collective-permute-start(bf16[520,128]{1,0:T(8,128)(2,1)S(1)} %get-tuple-element.15.refs_0_), channel_id=1, source_target_pairs={{0,16},{8,24},{16,32},{24,40},{32,48},{40,56},{48,0},{56,8},{1,17}... | collective-permute-start | bytes 399368 | tf_op jit(solution)/shard_map/ppermute | solution.py:263
  4.3 3.1 %collective-permute-start.1 = (bf16[520,128]{1,0:T(8,128)(2,1)S(1)}, bf16[520,128]{1,0:T(8,128)(2,1)S(1)}, u32[]{:S(2)}, u32[]{:S(2)}) collective-permute-start(bf16[520,128]{1,0:T(8,128)(2,1)S(1)} %get-tuple-element.15.refs_0_), channel_id=1, source_target_pairs={{0,48},{8,56},{16,0},{24,8},{32,16},{40,24},{48,32},{56,40},{1,49}... | collective-permute-start | bytes 399368 | tf_op jit(solution)/shard_map/ppermute | solution.py:263
  7.4 1.0 %copy.5 = bf16[4,256,128]{2,1,0:T(8,128)(2,1)S(1)} copy(bf16[4,256,128]{2,0,1:T(4,128)(2,1)} %bitcast.12) | data formatting | bytes 524288 | tf_op jit(solution)/shard_map/transpose | solution.py:268
  8.4 2.4 %collective-permute-start.8 = (bf16[1032,128]{1,0:T(8,128)(2,1)S(1)}, bf16[1032,128]{1,0:T(8,128)(2,1)S(1)}, u32[]{:S(2)}, u32[]{:S(2)}) collective-permute-start(bf16[1032,128]{1,0:T(8,128)(2,1)S(1)} %pad_maximum_fusion.2.refs_7_), channel_id=1, source_target_pairs={{128,0},{192,64},{129,1},{193,65},{130,2},{194,66},{131,3},{195,67... | collective-permute-start | bytes 792584 | tf_op jit(solution)/shard_map/ppermute | solution.py:263
  10.8 1.9 %collective-permute-start.6 = (bf16[1032,128]{1,0:T(8,128)(2,1)S(1)}, bf16[1032,128]{1,0:T(8,128)(2,1)S(1)}, u32[]{:S(2)}, u32[]{:S(2)}) collective-permute-start(bf16[1032,128]{1,0:T(8,128)(2,1)S(1)} %pad_maximum_fusion.2.refs_7_), channel_id=1, source_target_pairs={{64,0},{128,64},{192,128},{65,1},{129,65},{193,129},{66,2},{130,66... | collective-permute-start | bytes 792584 | tf_op jit(solution)/shard_map/ppermute | solution.py:263
  12.8 0.0 collective-permute-done.refs_1_
  12.8 2.1 %collective-permute-done.1.refs_2_ = bf16[520,128]{1,0:T(8,128)(2,1)S(1)} collective-permute-done((bf16[520,128]{1,0:T(8,128)(2,1)S(1)}, bf16[520,128]{1,0:T(8,128)(2,1)S(1)}, u32[]{:S(2)}, u32[]{:S(2)}) %collective-permute-start.1) | collective-permute-done | bytes 133152 | tf_op jit(solution)/shard_map/ppermute | solution.py:263
  14.9 0.1 collective-permute-start.2
  15.0 3.2 %collective-permute-start.3 = (bf16[1040,128]{1,0:T(8,128)(2,1)S(1)}, bf16[1040,128]{1,0:T(8,128)(2,1)S(1)}, u32[]{:S(2)}, u32[]{:S(2)}) collective-permute-start(bf16[1040,128]{1,0:T(8,128)(2,1)S(1)} %get-tuple-element.25), channel_id=1, source_target_pairs={{0,56},{8,0},{16,8},{24,16},{32,24},{40,32},{48,40},{56,48},{1,57}... | collective-permute-start | bytes 798728 | tf_op jit(solution)/shard_map/ppermute | solution.py:263
  18.2 1.6 %collective-permute-start.5 = (bf16[264,128]{1,0:T(8,128)(2,1)S(1)}, bf16[264,128]{1,0:T(8,128)(2,1)S(1)}, u32[]{:S(2)}, u32[]{:S(2)}) collective-permute-start(bf16[264,128]{1,0:T(8,128)(2,1)S(1)} %slice.9), channel_id=1, source_target_pairs={{0,48},{8,56},{16,0},{24,8},{32,16},{40,24},{48,32},{56,40},{1,49}... | collective-permute-start | bytes 202760 | tf_op jit(solution)/shard_map/ppermute | solution.py:263
  19.8 0.0 collective-permute-done.8.refs_3_.refs_4_
  19.8 1.4 %collective-permute-start.4 = (bf16[256,128]{1,0:T(8,128)(2,1)S(1)}, bf16[256,128]{1,0:T(8,128)(2,1)S(1)}, u32[]{:S(2)}, u32[]{:S(2)}) collective-permute-start(bf16[256,128]{1,0:T(8,128)(2,1)S(1)} %slice.8), channel_id=1, source_target_pairs={{0,16},{8,24},{16,32},{24,40},{32,48},{40,56},{48,0},{56,8},{1,17}... | collective-permute-start | bytes 196616 | tf_op jit(solution)/shard_map/ppermute | solution.py:263
  21.2 0.6 %shard_map.50 = (f32[1024,128]{1,0:T(8,128)S(1)}, f32[1024,128]{1,0:T(8,128)S(1)}, f32[1024,128]{1,0:T(8,128)S(1)}) custom-call(bf16[520,128]{1,0:T(8,128)(2,1)S(1)} %get-tuple-element.15.refs_0_, bf16[520,128]{1,0:T(8,128)(2,1)S(1)} %collective-permute-done.refs_1_, bf16[520,128]{1,0:T(8,128)(2,1)S(1)} %collective-permute-done.1.refs_2_, ...), custom_call_target="tpu_custom_call" | custom-call | flops 402653184 | bytes 1048576 | tf_op jit(solution)/shard_map/pallas_call | solution.py:199
  21.9 2.5 %collective-permute-done.6.refs_3_.refs_4_ = bf16[1032,128]{1,0:T(8,128)(2,1)S(1)} collective-permute-done((bf16[1032,128]{1,0:T(8,128)(2,1)S(1)}, bf16[1032,128]{1,0:T(8,128)(2,1)S(1)}, u32[]{:S(2)}, u32[]{:S(2)}) %collective-permute-start.6) | collective-permute-done | bytes 264224 | tf_op jit(solution)/shard_map/ppermute | solution.py:263
  24.4 2.4 %shard_map.48 = (f32[1024,128]{1,0:T(8,128)S(1)}, f32[1024,128]{1,0:T(8,128)S(1)}, f32[1024,128]{1,0:T(8,128)S(1)}) custom-call(bf16[520,128]{1,0:T(8,128)(2,1)S(1)} %get-tuple-element.15.refs_0_, bf16[520,128]{1,0:T(8,128)(2,1)S(1)} %collective-permute-done.refs_1_, bf16[520,128]{1,0:T(8,128)(2,1)S(1)} %collective-permute-done.1.refs_2_, ...), custom_call_target="tpu_custom_call" | custom-call | flops 402653184 | bytes 1048576 | tf_op jit(solution)/shard_map/pallas_call | solution.py:199
  26.8 0.0 collective-permute-done.4.refs_5_.refs_2_
  26.8 2.1 %collective-permute-done.5.refs_6_.refs_3_ = bf16[264,128]{1,0:T(8,128)(2,1)S(1)} collective-permute-done((bf16[264,128]{1,0:T(8,128)(2,1)S(1)}, bf16[264,128]{1,0:T(8,128)(2,1)S(1)}, u32[]{:S(2)}, u32[]{:S(2)}) %collective-permute-start.5) | collective-permute-done | bytes 67616 | tf_op jit(solution)/shard_map/ppermute | solution.py:263
  28.9 0.0 collective-permute-done.2.refs_3_.refs_0_
  28.9 0.0 collective-permute-done.3.refs_4_.refs_1_
  28.9 1.0 %shard_map.51 = bf16[1048,128]{1,0:T(8,128)(2,1)S(1)} custom-call(bf16[1040,128]{1,0:T(8,128)(2,1)S(1)} %collective-permute-done.2.refs_3_.refs_0_, bf16[1040,128]{1,0:T(8,128)(2,1)S(1)} %collective-permute-done.3.refs_4_.refs_1_, bf16[256,128]{1,0:T(8,128)(2,1)S(1)} %collective-permute-done.4.refs_5_.refs_2_, ...), custom_call_target="tpu_custom_call" | custom-call | flops 671088640 | bytes 1048576 | tf_op jit(solution)/shard_map/pallas_call | solution.py:199
  29.9 1.3 %collective-permute-start.9 = (bf16[1048,128]{1,0:T(8,128)(2,1)S(1)}, bf16[1048,128]{1,0:T(8,128)(2,1)S(1)}, u32[]{:S(2)}, u32[]{:S(2)}) collective-permute-start(bf16[1048,128]{1,0:T(8,128)(2,1)S(1)} %shard_map.51), channel_id=1, source_target_pairs={{0,128},{64,192},{1,129},{65,193},{2,130},{66,194},{3,131},{67,195... | collective-permute-start | bytes 804872 | tf_op jit(solution)/shard_map/ppermute | solution.py:263
  31.2 4.0 %shard_map.49 = bf16[1048,128]{1,0:T(8,128)(2,1)S(1)} custom-call(bf16[1040,128]{1,0:T(8,128)(2,1)S(1)} %collective-permute-done.2.refs_3_.refs_0_, bf16[1040,128]{1,0:T(8,128)(2,1)S(1)} %collective-permute-done.3.refs_4_.refs_1_, bf16[256,128]{1,0:T(8,128)(2,1)S(1)} %collective-permute-done.4.refs_5_.refs_2_, ...), custom_call_target="tpu_custom_call" | custom-call | flops 671088640 | bytes 1048576 | tf_op jit(solution)/shard_map/pallas_call | solution.py:199
  35.2 1.9 %collective-permute-start.7 = (bf16[1048,128]{1,0:T(8,128)(2,1)S(1)}, bf16[1048,128]{1,0:T(8,128)(2,1)S(1)}, u32[]{:S(2)}, u32[]{:S(2)}) collective-permute-start(bf16[1048,128]{1,0:T(8,128)(2,1)S(1)} %shard_map.49), channel_id=1, source_target_pairs={{0,64},{64,128},{128,192},{1,65},{65,129},{129,193},{2,66},{66,130... | collective-permute-start | bytes 804872 | tf_op jit(solution)/shard_map/ppermute | solution.py:263
  37.2 1.9 %shard_map.47 = (f32[1024,128]{1,0:T(8,128)S(1)}, f32[8,128]{1,0:T(8,128)S(1)}) custom-call(bf16[520,128]{1,0:T(8,128)(2,1)S(1)} %get-tuple-element.15.refs_0_, bf16[520,128]{1,0:T(8,128)(2,1)S(1)} %collective-permute-done.refs_1_, bf16[520,128]{1,0:T(8,128)(2,1)S(1)} %collective-permute-done.1.refs_2_, ...), custom_call_target="tpu_custom_call" | custom-call | flops 1073741824 | bytes 1048576 | tf_op jit(solution)/shard_map/pallas_call | solution.py:199
  39.0 3.3 %collective-permute-done.9.c_ref = bf16[1048,128]{1,0:T(8,128)(2,1)S(1)} collective-permute-done((bf16[1048,128]{1,0:T(8,128)(2,1)S(1)}, bf16[1048,128]{1,0:T(8,128)(2,1)S(1)}, u32[]{:S(2)}, u32[]{:S(2)}) %collective-permute-start.9) | collective-permute-done | bytes 268320 | tf_op jit(solution)/shard_map/ppermute | solution.py:263
  42.4 3.2 %collective-permute-done.7.b_ref = bf16[1048,128]{1,0:T(8,128)(2,1)S(1)} collective-permute-done((bf16[1048,128]{1,0:T(8,128)(2,1)S(1)}, bf16[1048,128]{1,0:T(8,128)(2,1)S(1)}, u32[]{:S(2)}, u32[]{:S(2)}) %collective-permute-start.7) | collective-permute-done | bytes 268320 | tf_op jit(solution)/shard_map/ppermute | solution.py:263
  45.6 0.7 %shard_map.52 = bf16[256,512]{1,0:T(8,128)(2,1)S(1)} custom-call(f32[1024,128]{1,0:T(8,128)S(1)} %get-tuple-element.17.a_ref, f32[8,128]{1,0:T(8,128)S(1)} %get-tuple-element.18.lse_ref, bf16[1048,128]{1,0:T(8,128)(2,1)S(1)} %collective-permute-done.7.b_ref, bf16[1048,128]{1,0:T(8,128)(2,1)S(1)} %collective-permute-done.9.c_ref), custom_call_target="tpu_custom_call" | custom-call | tf_op jit(solution)/shard_map/pallas_call | solution.py:250
  46.3 11.8 %all_to_all.19 = bf16[8,32,512]{2,1,0:T(8,128)(2,1)S(1)} all-to-all(bf16[8,32,512]{2,1,0:T(8,128)(2,1)S(1)} %bitcast.9), channel_id=1, replica_groups=mesh['x'=4,'z'=8,'y'=4,'core'=2] {'y','core'}, dimensions={0} | all-to-all | bytes 524288 | tf_op jit(solution)/shard_map/all_to_all | solution.py:288
  58.0 0.7 %copy.7 = bf16[8,4,8,512]{3,2,0,1:T(8,128)(2,1)} copy(bf16[8,4,8,512]{3,2,1,0:T(8,128)(2,1)S(1)} %bitcast.11) | data formatting | bytes 524288 | tf_op jit(solution)/shard_map/all_to_all | solution.py:288
  (4 shorter events, 0.1 us)
Async XLA Ops:
  0.9 11.9 %collective-permute-start = (bf16[520,128]{1,0:T(8,128)(2,1)S(1)}, bf16[520,128]{1,0:T(8,128)(2,1)S(1)}, u32[]{:S(2)}, u32[]{:S(2)}) collective-permute-start(bf16[520,128]{1,0:T(8,128)(2,1)S(1)} %get-tuple-element.15.refs_0_), channel_id=1, source_target_pairs={{0,16},{8,24},{16,32},{24,40},{32,48},{40,56},{48,0},{56,8},{1,17}... | collective-permute-start | bytes 399368 | tf_op jit(solution)/shard_map/ppermute | solution.py:263
  4.3 10.6 %collective-permute-start.1 = (bf16[520,128]{1,0:T(8,128)(2,1)S(1)}, bf16[520,128]{1,0:T(8,128)(2,1)S(1)}, u32[]{:S(2)}, u32[]{:S(2)}) collective-permute-start(bf16[520,128]{1,0:T(8,128)(2,1)S(1)} %get-tuple-element.15.refs_0_), channel_id=1, source_target_pairs={{0,48},{8,56},{16,0},{24,8},{32,16},{40,24},{48,32},{56,40},{1,49}... | collective-permute-start | bytes 399368 | tf_op jit(solution)/shard_map/ppermute | solution.py:263
  8.4 11.4 %collective-permute-start.8 = (bf16[1032,128]{1,0:T(8,128)(2,1)S(1)}, bf16[1032,128]{1,0:T(8,128)(2,1)S(1)}, u32[]{:S(2)}, u32[]{:S(2)}) collective-permute-start(bf16[1032,128]{1,0:T(8,128)(2,1)S(1)} %pad_maximum_fusion.2.refs_7_), channel_id=1, source_target_pairs={{128,0},{192,64},{129,1},{193,65},{130,2},{194,66},{131,3},{195,67... | collective-permute-start | bytes 792584 | tf_op jit(solution)/shard_map/ppermute | solution.py:263
  10.8 13.6 %collective-permute-start.6 = (bf16[1032,128]{1,0:T(8,128)(2,1)S(1)}, bf16[1032,128]{1,0:T(8,128)(2,1)S(1)}, u32[]{:S(2)}, u32[]{:S(2)}) collective-permute-start(bf16[1032,128]{1,0:T(8,128)(2,1)S(1)} %pad_maximum_fusion.2.refs_7_), channel_id=1, source_target_pairs={{64,0},{128,64},{192,128},{65,1},{129,65},{193,129},{66,2},{130,66... | collective-permute-start | bytes 792584 | tf_op jit(solution)/shard_map/ppermute | solution.py:263
  14.9 14.0 %collective-permute-start.2 = (bf16[1040,128]{1,0:T(8,128)(2,1)S(1)}, bf16[1040,128]{1,0:T(8,128)(2,1)S(1)}, u32[]{:S(2)}, u32[]{:S(2)}) collective-permute-start(bf16[1040,128]{1,0:T(8,128)(2,1)S(1)} %get-tuple-element.26), channel_id=1, source_target_pairs={{0,8},{8,16},{16,24},{24,32},{32,40},{40,48},{48,56},{56,0},{1,9},... | collective-permute-start | bytes 798728 | tf_op jit(solution)/shard_map/ppermute | solution.py:263
  15.0 13.9 %collective-permute-start.3 = (bf16[1040,128]{1,0:T(8,128)(2,1)S(1)}, bf16[1040,128]{1,0:T(8,128)(2,1)S(1)}, u32[]{:S(2)}, u32[]{:S(2)}) collective-permute-start(bf16[1040,128]{1,0:T(8,128)(2,1)S(1)} %get-tuple-element.25), channel_id=1, source_target_pairs={{0,56},{8,0},{16,8},{24,16},{32,24},{40,32},{48,40},{56,48},{1,57}... | collective-permute-start | bytes 798728 | tf_op jit(solution)/shard_map/ppermute | solution.py:263
  18.2 10.7 %collective-permute-start.5 = (bf16[264,128]{1,0:T(8,128)(2,1)S(1)}, bf16[264,128]{1,0:T(8,128)(2,1)S(1)}, u32[]{:S(2)}, u32[]{:S(2)}) collective-permute-start(bf16[264,128]{1,0:T(8,128)(2,1)S(1)} %slice.9), channel_id=1, source_target_pairs={{0,48},{8,56},{16,0},{24,8},{32,16},{40,24},{48,32},{56,40},{1,49}... | collective-permute-start | bytes 202760 | tf_op jit(solution)/shard_map/ppermute | solution.py:263
  19.8 7.0 %collective-permute-start.4 = (bf16[256,128]{1,0:T(8,128)(2,1)S(1)}, bf16[256,128]{1,0:T(8,128)(2,1)S(1)}, u32[]{:S(2)}, u32[]{:S(2)}) collective-permute-start(bf16[256,128]{1,0:T(8,128)(2,1)S(1)} %slice.8), channel_id=1, source_target_pairs={{0,16},{8,24},{16,32},{24,40},{32,48},{40,56},{48,0},{56,8},{1,17}... | collective-permute-start | bytes 196616 | tf_op jit(solution)/shard_map/ppermute | solution.py:263
  29.9 12.5 %collective-permute-start.9 = (bf16[1048,128]{1,0:T(8,128)(2,1)S(1)}, bf16[1048,128]{1,0:T(8,128)(2,1)S(1)}, u32[]{:S(2)}, u32[]{:S(2)}) collective-permute-start(bf16[1048,128]{1,0:T(8,128)(2,1)S(1)} %shard_map.51), channel_id=1, source_target_pairs={{0,128},{64,192},{1,129},{65,193},{2,130},{66,194},{3,131},{67,195... | collective-permute-start | bytes 804872 | tf_op jit(solution)/shard_map/ppermute | solution.py:263
  35.2 10.4 %collective-permute-start.7 = (bf16[1048,128]{1,0:T(8,128)(2,1)S(1)}, bf16[1048,128]{1,0:T(8,128)(2,1)S(1)}, u32[]{:S(2)}, u32[]{:S(2)}) collective-permute-start(bf16[1048,128]{1,0:T(8,128)(2,1)S(1)} %shard_map.49), channel_id=1, source_target_pairs={{0,64},{64,128},{128,192},{1,65},{65,129},{129,193},{2,66},{66,130... | collective-permute-start | bytes 804872 | tf_op jit(solution)/shard_map/ppermute | solution.py:263
